TPU v7x, 32 devices: a whole 2x2x4 slice. The times are simulated.
32 devices in a mesh: pairs: 8 (over z, x), grp: 4 (over y, core).
Axes of the slice: x: 2, y: 2, z: 4, core: 2. Of those that a mesh axis runs over, the one named last changes fastest.
Arguments:
- coefficients: bfloat16 [128, 512, 128], P('pairs', 'grp'), may hold values from -0.4140625 to 0.4140625
- domain: int32 [128, 512], P('pairs', 'grp'), may hold values from 0 to 767, as said below
- coupling_owner: int32 [128, 8], P('pairs'), may hold values from 0 to 7, all different within a row; in each aligned block of 16 rows (0 to 15, 16 to 31, ...) at most 16 rows name the same one
- coupling_slot: int32 [128, 8], P('pairs'), may hold values from 0 to 15
- coupling_fock: float32 [128, 8], P('pairs'), may hold values from -0.5 to 0.5
- exchange_integrals: float32 [128, 128, 128], P('pairs'), may hold values from -6 to 6
- pno_energy: float32 [128, 128], P('pairs'), may hold values from 0.3 to 3
- pair_shift: float32 [128], P('pairs'), may hold values from 0.4 to 2
- amplitudes_start: float32 [128, 128, 128], P('pairs'), may hold values from -1.8 to 1.8
Outputs:
- amplitudes: float32 [128, 128, 128], P('pairs')
Inputs may be any that keep to these rules, and one draw needn't show every extreme that they name: `coupling_owner`: each row names different indices. Among the 16 rows of one index of pairs no value is named more than 16 times, a bound that some block reaches. `domain`: for each pair and each g from 0 to 3, the entries g * 128 to (g + 1) * 128 - 1 are distinct numbers from g * 192 to (g + 1) * 192 - 1.
All inputs are finite; a program needn't handle non-finite values.
Results may differ from a plain program's by a relative error of at most 0.0025.
Values may be sent and summed in bfloat16 or wider, within the bound.
A program may use at most 128 MiB of HBM per device.

v0:
```python
import functools

import jax
import jax.numpy as jnp
from jax import lax
from jax.experimental import pallas as pl
from jax.experimental.pallas import tpu as pltpu
from jax.sharding import PartitionSpec as P

NB = 192
MESH = pl.DeviceIdType.MESH
F32, BF16 = jnp.float32, jnp.bfloat16


def ring_position(rank, n):
    odd = rank % 2
    return (1 - odd) * (rank // 2) + odd * (n - 1 - rank // 2)


def ring_rank(position, n):
    back = position // (n // 2)
    return (1 - back) * 2 * position + back * (2 * (n - 1 - position) + 1)


def places(n):
    p, g = lax.axis_index("pairs"), lax.axis_index("grp")
    position = ring_position(p, n)
    core, half = g % 2, g // 2
    mate = 2 * half + (1 - core)
    across = 2 * (1 - half) + core
    return p, g, position, mate, across


def at(position, n):
    return ring_rank((position + n) % n, n)


def greet(peers):
    barrier = pltpu.get_barrier_semaphore()
    for peer in peers:
        pl.semaphore_signal(barrier, inc=1, device_id=peer, device_id_type=MESH)
    pl.semaphore_wait(barrier, len(peers))


def remote(src, dst, send, recv, peer):
    return pltpu.make_async_remote_copy(
        src_ref=src, dst_ref=dst, send_sem=send, recv_sem=recv, device_id=peer, device_id_type=MESH
    )


def ring_parts(steps, parts):
    def of(step, direction):
        if step < steps:
            return tuple(range(parts))
        return tuple(c for c in range(parts) if c % 2 == direction)

    return of


def intersections(
    n, slot_ref, c_ref, dom_ref, out_ref,
    cbuf, dbuf, turned, wide, own, msend, mrecv, ysend, yrecv, keep,
    rs, rr, ms, mr, ys, yr,
):
    p, g, position, mate, across = places(n)
    pc = c_ref.shape[0]
    quarter = pc // 4
    rows = c_ref.shape[1]
    steps = n // 2
    right, left = at(position + 1, n), at(position - 1, n)
    ring_peer = (lambda r: (r, g))
    peers = [(right, g), (left, g), (p, mate), (p, across)]
    greet(peers)
    parts_of = ring_parts(steps, 3)
    hp = pc // 2

    def part(ref_c, ref_d, c):
        if c == 2:
            return ref_d
        return ref_c.at[pl.ds(c * hp, hp)]

    def move(step, direction, c):
        offset = -(step - 1) if direction == 0 else step - 1
        rank = at(position + offset, n)
        if step == 1:
            src = part(c_ref, dom_ref, c)
        else:
            src = part(cbuf.at[rank], dbuf.at[rank], c)
        dst = part(cbuf.at[rank], dbuf.at[rank], c)
        return remote(
            src, dst, rs.at[direction, step - 1, c], rr.at[direction, step - 1, c],
            ring_peer(right if direction == 0 else left),
        )

    def arrive(step, direction, c):
        offset = -step if direction == 0 else step
        rank = at(position + offset, n)
        dst = part(cbuf.at[rank], dbuf.at[rank], c)
        remote(
            dst, dst, rs.at[direction, step - 1, c], rr.at[direction, step - 1, c],
            ring_peer(left if direction == 0 else right),
        ).wait_recv()

    for c in (2, 0, 1):
        for d in (0, 1):
            if c in parts_of(1, d):
                move(1, d, c).start()

    base = g * NB
    lines = lax.broadcasted_iota(jnp.int32, (NB, rows), 0)
    core, half = g % 2, g // 2

    def expand(block, doms):
        def one(s, carry):
            hit = (lines == (doms[pl.ds(s, 1), :] - base)).astype(F32).astype(BF16)
            wide[s] = jnp.dot(hit, block[s], preferred_element_type=F32).astype(BF16)
            return carry

        lax.fori_loop(0, pc, one, 0, unroll=8)

    def mate_copy(k, rank):
        return remote(msend.at[k % 2], mrecv.at[rank], ms.at[k], mr.at[k], (p, mate))

    def across_copy(k, rank):
        return remote(ysend.at[k % 2], yrecv.at[rank], ys.at[k], yr.at[k], (p, across))

    ranks = []

    def product(t, rank):
        return jnp.dot(turned[t], wide[slot_ref[t, rank]], preferred_element_type=F32)

    def links(k, rank):
        if k >= 2:
            mate_copy(k - 2, ranks[k - 2]).wait_send()

        def theirs(i, carry):
            t = (2 * (i // quarter) + 1 - core) * quarter + i % quarter
            msend[k % 2, i] = product(t, rank)
            return carry

        lax.fori_loop(0, 2 * quarter, theirs, 0, unroll=8)
        mate_copy(k, rank).start()

        def ours(i, carry):
            t = (2 * (i // quarter) + core) * quarter + i % quarter
            own[k % 2, i] = product(t, rank)
            return carry

        lax.fori_loop(0, 2 * quarter, ours, 0, unroll=8)

    def finish(k):
        rank = ranks[k]
        if k >= 2:
            across_copy(k - 2, ranks[k - 2]).wait_send()
        mate_copy(k, rank).wait_recv()

        def send(j, carry):
            i = (1 - half) * quarter + j
            ysend[k % 2, j] = own[k % 2, i] + mrecv[rank, i]
            return carry

        lax.fori_loop(0, quarter, send, 0)
        across_copy(k, rank).start()

        def hold(j, carry):
            i = half * quarter + j
            keep[rank, j] = own[k % 2, i] + mrecv[rank, i]
            return carry

        lax.fori_loop(0, quarter, hold, 0)

    def process(rank):
        k = len(ranks)
        ranks.append(rank)
        links(k, rank)

    expand(c_ref, dom_ref)

    def turn(t, carry):
        turned[t] = wide[t].astype(F32).T.astype(BF16)
        return carry

    lax.fori_loop(0, pc, turn, 0, unroll=2)
    process(p)
    finish(0)
    for step in range(1, steps + 1):
        for c in (2, 0, 1):
            for d in (0, 1):
                if c in parts_of(step, d):
                    arrive(step, d, c)
                if step < steps and c in parts_of(step + 1, d):
                    move(step + 1, d, c).start()
        if step == steps - 1:
            yield None
        for d in (0, 1) if step < steps else (0,):
            rank = at(position + (-step if d == 0 else step), n)
            expand(cbuf.at[rank], dbuf.at[rank])
            process(rank)
            if d == 1:
                finish(len(ranks) - 2)
        finish(len(ranks) - 1)
    def settle(k):
        rank = ranks[k]
        across_copy(k, rank).wait_recv()

        def last(j, carry):
            out_ref[rank, j] = (keep[rank, j] + yrecv[rank, j]).astype(BF16)
            return carry

        lax.fori_loop(0, quarter, last, 0)

    yield settle
    for k in (n - 2, n - 1):
        mate_copy(k, ranks[k]).wait_send()
        across_copy(k, ranks[k]).wait_send()
    for step in range(1, steps + 1):
        for d in (0, 1):
            for c in parts_of(step, d):
                move(step, d, c).wait_send()


def iteration(
    n, first, joined, alone, slot_ref, fock_ref, start_ref, x_ref, k_ref, e_ref, out_ref,
    abuf, stage, acc, mine, rs, rr, ms, mr, ys, yr, fs, fr,
):
    p, g, position, mate, across = places(n)
    pc = k_ref.shape[0]
    width = k_ref.shape[1]
    quarter = pc // 4
    eighth = quarter // 2
    steps = n // 2
    right, left = at(position + 1, n), at(position - 1, n)
    diagonal = 3 - g
    if alone:
        greet([(right, g), (left, g), (p, mate), (p, across)])
    parts = 4 if joined else 3
    parts_of = ring_parts(steps, parts)

    def chunk(rank, group, c):
        return abuf.at[pl.ds(rank * pc + group * quarter + (c % 2) * eighth, eighth)]

    def span(rank, c):
        return chunk(rank, g if c < 2 else across, c)

    def ring_copy(step, direction, c):
        offset = -(step - 1) if direction == 0 else step - 1
        ref = span(at(position + offset, n), c)
        src = ref
        if step == 1 and c < 2 and not first:
            src = start_ref.at[pl.ds(c * eighth, eighth)]
        return remote(
            src, ref, rs.at[direction, step - 1, c], rr.at[direction, step - 1, c],
            (right if direction == 0 else left, g),
        )

    def arrive(step, direction, c):
        offset = -step if direction == 0 else step
        ref = span(at(position + offset, n), c)
        remote(
            ref, ref, rs.at[direction, step - 1, c], rr.at[direction, step - 1, c],
            (left if direction == 0 else right, g),
        ).wait_recv()

    def mate_copy(k, rank, c, src=None):
        ref = span(rank, c)
        return remote(ref if src is None else src, ref, ms.at[k, c], mr.at[k, c], (p, mate))

    def mate_wait(k, rank):
        for c in range(4):
            ref = chunk(rank, mate if c < 2 else diagonal, c)
            remote(ref, ref, ms.at[k, c], mr.at[k, c], (p, mate)).wait_recv()

    def across_copy(k, rank, c=1, src=None):
        ref = span(rank, c)
        sem = k if c == 1 else n
        return remote(ref if src is None else src, ref, ys.at[sem], yr.at[sem], (p, across))

    def across_wait(k, rank, c=3):
        ref = span(rank, c)
        sem = k if c == 3 else n
        remote(ref, ref, ys.at[sem], yr.at[sem], (p, across)).wait_recv()

    def own_half(c):
        return start_ref.at[pl.ds(c * eighth, eighth)]

    if first:
        def copy_own(i, carry):
            abuf[p * pc + i] = start_ref[i].astype(BF16)
            return carry

        def group_in(group):
            lax.fori_loop(group * quarter, (group + 1) * quarter, copy_own, 0)

        group_in(g)
        for c in (0, 1):
            for d in (0, 1):
                if c in parts_of(1, d):
                    ring_copy(1, d, c).start()
        group_in(across)
        for c in range(2, parts):
            for d in (0, 1):
                if c in parts_of(1, d):
                    ring_copy(1, d, c).start()
        group_in(mate)
        group_in(diagonal)
    else:
        for c in (0, 1):
            across_copy(0, p, c, own_half(c)).start()
            for d in (0, 1):
                if c in parts_of(1, d):
                    ring_copy(1, d, c).start()
        for c in (0, 1):
            mate_copy(0, p, c, own_half(c)).start()

        def copy_own(i, carry):
            abuf[p * pc + g * quarter + i] = start_ref[i]
            return carry

        lax.fori_loop(0, quarter, copy_own, 0)
        across_wait(0, p, 2)
        for d in (0, 1):
            if 2 in parts_of(1, d):
                ring_copy(1, d, 2).start()
        mate_copy(0, p, 2).start()
        across_wait(0, p, 3)
        mate_copy(0, p, 3).start()
        mate_wait(0, p)

    settle = yield None
    acc[...] = jnp.zeros_like(acc)

    def couple(rank, k):
        if settle is not None:
            settle(k)

        def copy(i, carry):
            stage[i] = abuf[rank * pc + i]
            return carry

        lax.fori_loop(0, pc, copy, 0, unroll=4)

        def one(j, carry):
            t = g * quarter + j
            source = stage[slot_ref[t, rank]]
            x = x_ref[rank, j]
            h = jnp.dot(x, source, preferred_element_type=F32).astype(BF16)
            y = lax.dot_general(h, x, (((1,), (1,)), ((), ())), preferred_element_type=F32)
            acc[j] += fock_ref[t, rank] * y
            return carry

        lax.fori_loop(0, quarter, one, 0, unroll=4)

    couple(p, 0)

    def exchange(blocks):
        for k, rank in () if joined else blocks:
            across_wait(k, rank)
            mate_copy(k, rank, 3).start()

    def use(blocks):
        for k, rank in blocks:
            mate_wait(k, rank)
            couple(rank, k)

    landed, shared = [], []
    for step in range(1, steps + 1):
        for c in (1, 0, 2, 3)[:parts]:
            for d in (0, 1):
                rank = at(position + (-step if d == 0 else step), n)
                if c in parts_of(step, d):
                    arrive(step, d, c)
                    if step < steps and c in parts_of(step + 1, d):
                        ring_copy(step + 1, d, c).start()
                    k = 2 * step - 1 + (d if step < steps else 0)
                    if c == 1 and not joined:
                        across_copy(k, rank).start()
                    mate_copy(k, rank, c).start()
        exchange(landed)
        use(shared)
        shared = landed
        landed = [
            (2 * step - 1 + d, at(position + (-step if d == 0 else step), n))
            for d in ((0, 1) if step < steps else (0,))
        ]
    exchange(landed)
    use(shared)
    use(landed)

    def scaled(j):
        t = g * quarter + j
        row = jnp.broadcast_to(e_ref[pl.ds(t, 1), :], (width, width))
        return (-(k_ref[t] + acc[j]) / (row.T + row + fock_ref[t, n])).astype(BF16)

    if first:
        def result(j, carry):
            out_ref[j] = scaled(j)
            return carry

        lax.fori_loop(0, quarter, result, 0, unroll=2)
    else:
        def block(ref, group):
            return ref.at[pl.ds(group * quarter, quarter)]

        def result(j, carry):
            value = scaled(j)
            mine[j] = value
            out_ref[g * quarter + j] = value
            return carry

        lax.fori_loop(0, quarter, result, 0, unroll=2)
        over = remote(mine, block(out_ref, g), fs.at[0], fr.at[0], (p, across))
        beside = remote(mine, block(out_ref, g), fs.at[1], fr.at[1], (p, mate))
        corner = remote(
            block(out_ref, across), block(out_ref, across), fs.at[2], fr.at[2], (p, mate)
        )
        over.start()
        beside.start()
        remote(mine, block(out_ref, across), fs.at[0], fr.at[0], (p, across)).wait_recv()
        corner.start()
        remote(mine, block(out_ref, mate), fs.at[1], fr.at[1], (p, mate)).wait_recv()
        remote(mine, block(out_ref, diagonal), fs.at[2], fr.at[2], (p, mate)).wait_recv()
        over.wait_send()
        beside.wait_send()
        corner.wait_send()
        across_copy(0, p, 0, own_half(0)).wait_send()
        across_copy(0, p, 1, own_half(1)).wait_send()
        for c in range(4):
            mate_copy(0, p, c).wait_send()
    for k in range(1, n):
        if not joined:
            across_copy(k, p).wait_send()
        for c in range(4):
            mate_copy(k, p, c).wait_send()
    for step in range(1, steps + 1):
        for d in (0, 1):
            for c in parts_of(step, d):
                ring_copy(step, d, c).wait_send()


def intersections_alone(*args):
    steps = intersections(*args)
    next(steps)
    settle = next(steps)
    for k in range(args[0]):
        settle(k)
    next(steps, None)


def iteration_alone(n, first, *args):
    steps = iteration(n, first, False, True, *args)
    next(steps)
    try:
        steps.send(None)
    except StopIteration:
        pass


def opening(
    n, made, slot_ref, fock_ref, c_ref, dom_ref, start_ref, k_ref, e_ref, out_ref,
    x_ref, amp_ref, *scratch
):
    used = made + (len(scratch) - made) // 2
    blocks = intersections(n, slot_ref, c_ref, dom_ref, x_ref, *scratch[:made])
    next(blocks)
    amps = iteration(
        n, True, True, False, slot_ref, fock_ref, start_ref, x_ref, k_ref, e_ref, amp_ref,
        *scratch[made:used],
    )
    next(amps)
    settle = next(blocks)
    try:
        amps.send(settle)
    except StopIteration:
        pass
    amps = iteration(
        n, False, False, False, slot_ref, fock_ref, amp_ref, x_ref, k_ref, e_ref, out_ref,
        *scratch[used:],
    )
    next(amps)
    try:
        amps.send(None)
    except StopIteration:
        pass
    next(blocks, None)


def on_device(
    coefficients, domain, coupling_owner, coupling_slot, coupling_fock,
    exchange_integrals, pno_energy, pair_shift, amplitudes_start,
):
    n = lax.axis_size("pairs")
    pc, rows, width = coefficients.shape
    quarter = pc // lax.axis_size("grp")
    steps = n // 2
    named = coupling_owner[:, :, None] == jnp.arange(n, dtype=jnp.int32)[None, None, :]
    slots = jnp.sum(jnp.where(named, coupling_slot[:, :, None], 0), axis=1)
    focks = jnp.sum(jnp.where(named, coupling_fock[:, :, None], 0.0), axis=1)
    focks = jnp.concatenate([focks, pair_shift[:, None]], axis=1)
    vmem, smem = pl.BlockSpec(memory_space=pltpu.VMEM), pl.BlockSpec(memory_space=pltpu.SMEM)
    dma = pltpu.SemaphoreType.DMA

    def params(collective):
        return pltpu.CompilerParams(
            collective_id=collective, has_side_effects=True, vmem_limit_bytes=60 * 2**20
        )

    big = (width, width)
    x_shape = jax.ShapeDtypeStruct((n, quarter, *big), BF16)
    block_scratch = [
        pltpu.VMEM((n, pc, rows, width), BF16),
        pltpu.VMEM((n, pc, rows), jnp.int32),
        pltpu.VMEM((pc, width, NB), BF16),
        pltpu.VMEM((pc, NB, width), BF16),
        pltpu.VMEM((2, 2 * quarter, *big), F32),
        pltpu.VMEM((2, 2 * quarter, *big), F32),
        pltpu.VMEM((n, 2 * quarter, *big), F32),
        pltpu.VMEM((2, quarter, *big), F32),
        pltpu.VMEM((n, quarter, *big), F32),
        pltpu.VMEM((n, quarter, *big), F32),
        dma((2, steps, 3)), dma((2, steps, 3)),
        dma((n,)), dma((n,)), dma((n,)), dma((n,)),
    ]
    amp_scratch = [
        pltpu.VMEM((n * pc, *big), BF16),
        pltpu.VMEM((pc, *big), BF16),
        pltpu.VMEM((quarter, *big), F32),
        pltpu.VMEM((quarter, *big), BF16),
        dma((2, steps, 4)), dma((2, steps, 4)),
        dma((n, 4)), dma((n, 4)), dma((n + 1,)), dma((n + 1,)), dma((3,)), dma((3,)),
    ]
    half_shape = jax.ShapeDtypeStruct((quarter, *big), BF16)

    def iterate(first, start, x):
        return pl.pallas_call(
            functools.partial(iteration_alone, n, first),
            out_shape=half_shape if first else jax.ShapeDtypeStruct((pc, *big), BF16),
            in_specs=[smem, smem, vmem, vmem, vmem, vmem],
            out_specs=vmem,
            scratch_shapes=amp_scratch,
            compiler_params=params(1 if first else 2),
            name="first" if first else "second",
        )(slots, focks, start, x, exchange_integrals, pno_energy)

    held = n * width * (2 * pc * (rows + width) + 4 * width * 4 * quarter + 2 * width * quarter)
    if held < 40 * 2**20:
        return pl.pallas_call(
            functools.partial(opening, n, len(block_scratch)),
            out_shape=jax.ShapeDtypeStruct((pc, *big), BF16),
            in_specs=[smem, smem, vmem, vmem, vmem, vmem, vmem],
            out_specs=vmem,
            scratch_shapes=[
                pltpu.VMEM(x_shape.shape, BF16), pltpu.VMEM(half_shape.shape, BF16),
                *block_scratch, *amp_scratch, *amp_scratch,
            ],
            compiler_params=params(0),
            name="amplitudes",
        )(slots, focks, coefficients, domain, amplitudes_start, exchange_integrals, pno_energy).astype(F32)
    else:
        x = pl.pallas_call(
            functools.partial(intersections_alone, n),
            out_shape=x_shape,
            in_specs=[smem, vmem, vmem],
            out_specs=vmem,
            scratch_shapes=block_scratch,
            compiler_params=params(0),
            name="intersections",
        )(slots, coefficients, domain)
        amps = iterate(True, amplitudes_start, x)
    return iterate(False, amps, x).astype(F32)


def solution(mesh):
    placed = (
        P("pairs", "grp", None),
        P("pairs", "grp"),
        P("pairs", None),
        P("pairs", None),
        P("pairs", None),
        P("pairs", None, None),
        P("pairs", None),
        P("pairs"),
        P("pairs", None, None),
    )
    return jax.shard_map(
        on_device, mesh=mesh, in_specs=placed, out_specs=P("pairs", None, None), check_vma=False
    )
```

profile of v0, /device:TPU:0, one launch (start us, length us, event | category | flops | bytes accessed | tf_op | source)
XLA Modules:
  0.0 111.7 jit_solution(3240286529966865701)
XLA Ops:
  0.0 0.7 select_reduce_fusion.1
  0.7 0.0 copy-start
  0.7 0.0 copy-start.1
  0.7 0.7 copy.16.slot_ref
  1.4 0.0 copy-done
  1.4 0.0 copy-done.1
  1.4 0.0 copy-start.2
  1.4 0.1 copy.14
  1.5 0.6 copy-done.2
  2.1 0.1 copy.15
  2.2 0.7 pad_maximum_fusion.fock_ref
  2.8 106.7 %amplitudes.1 = bf16[16,128,128]{2,1,0:T(8,128)(2,1)} custom-call(s32[16,8]{1,0:T(8,128)} %copy.16.slot_ref, f32[16,9]{1,0:T(8,128)} %pad_maximum_fusion.fock_ref, bf16[16,128,128]{2,1,0:T(8,128)(2,1)} %c_ref.1, s32[16,128]{1,0:T(8,128)} %dom_ref.1, f32[16,128,128]{2,1,0:T(8,128)} %start_ref.1, f32[16,128,128]{2,1,0:T(8,128)} %k_ref.1, f32[16,128]{1,0:T(8,128)} %e_ref.1), custom_call_target="tpu_custom_call" | custom-call | tf_op jit(solution)/shard_map/amplitudes/pallas_call | solution.py:546
  109.5 2.1 %convert_element_type.3 = f32[16,128,128]{2,1,0:T(8,128)} convert(bf16[16,128,128]{2,1,0:T(8,128)(2,1)} %amplitudes.1) | non-fusion elementwise | flops 262144 | bytes 1572864 | tf_op jit(solution)/shard_map/convert_element_type | solution.py:557
  (1 shorter events, 0.0 us)
Async XLA Ops:
  0.7 0.7 copy-start
  0.7 0.7 copy-start.1
  1.4 0.7 copy-start.2
where the time goes:
time: 112 us
  Pallas kernels  107 us (96%)
  other arithmetic  3.52 us (3%)
  local copies, waits for them, and re-layouts  1.42 us (1%)
    pallas_call x1, Pallas kernels, on_device(): pl.pallas_call(functools.partial(opening, n, len(block_scratch)), out_sha...  107 us

commit v1 on v0

--- a/solution.py
+++ b/solution.py
@@ -484,6 +484,564 @@
     next(blocks, None)
 
 
+class Wires:
+    def __init__(self, send, recv, here):
+        self.send, self.recv, self.here = send, recv, here
+        self.ids, self.started = {}, []
+
+    def link(self, key, src, dst, peer):
+        at_key = self.ids.setdefault(key, len(self.ids))
+        return remote(src, dst, self.send.at[at_key], self.recv.at[at_key], peer)
+
+    def start(self, key, src, dst, peer, when=None):
+        copy = self.link(key, src, dst, peer)
+        if when is None:
+            copy.start()
+        else:
+            pl.when(when)(copy.start)
+        self.started.append((key, src, dst, peer, when))
+
+    def start_in(self, when, key, src, dst, peer):
+        copy = self.link(key, src, dst, peer)
+        copy.start()
+        self.started.append((key, src, dst, peer, when))
+
+    def start_all(self, when, jobs):
+        def run():
+            for key, src, dst, peer in jobs:
+                self.start_in(when, key, src, dst, peer)
+
+        pl.when(when)(run)
+
+    def wait(self, key, dst, when=None):
+        copy = self.link(key, dst, dst, self.here)
+        if when is None:
+            copy.wait_recv()
+        else:
+            pl.when(when)(copy.wait_recv)
+
+    def drain(self):
+        for *what, when in self.started:
+            copy = self.link(*what)
+            if when is None:
+                copy.wait_send()
+            else:
+                pl.when(when)(copy.wait_send)
+
+
+def note(*what):
+    return None
+
+
+def quadrants(
+    n, owner_ref, slot_ref, fock_ref, shift_ref, c_ref, dom_ref, start_ref, k_ref, e_ref, out_ref,
+    src, dom, blocks, bdom, bslot, bfock, wide, turned, x, start, k_own, amps_a, amps_b, amps_c, amps_d,
+    acc, yout, yx, ysum, yin, mine, send, recv, local,
+):
+    p, g = lax.axis_index("pairs"), lax.axis_index("grp")
+    pc, rows, width = c_ref.shape
+    quarter = pc // 4
+    half_quarter = quarter // 2
+    layers = n // 2
+    layer, column = p // 2, p % 2
+    inner = (layer % 2 + layer // 2) % 2
+    mid, end = inner == 1, inner == 0
+    partner = (layer + 1 - 2 * (layer % 2)) * 2 + column
+    cross = (layers - 1 - layer) * 2 + column
+    far = ((layer + layers // 2) % layers) * 2 + column
+    beside = layer * 2 + 1 - column
+    groups = (g, g + 1 - 2 * (g % 2), (g + 2) % 4, 3 - g)
+    _, mate, across, diagonal = groups
+    to_mate, to_across = (p, mate), (p, across)
+    to_partner, to_cross, to_beside, to_far = (partner, g), (cross, g), (beside, g), (far, g)
+    wires = Wires(send, recv, to_mate)
+    amps = ((amps_a, amps_b), (amps_c, amps_d))
+    wires.mid = mid
+
+    barrier = pltpu.get_barrier_semaphore()
+
+    def hello(peer):
+        pl.semaphore_signal(barrier, inc=1, device_id=peer, device_id_type=MESH)
+
+    for peer in (to_far, to_partner, to_beside, to_across, to_mate):
+        hello(peer)
+    pl.when(mid)(lambda: hello(to_cross))
+
+    load_start = pltpu.make_async_copy(start_ref, start, local.at[0])
+    load_start.start()
+    load_k = pltpu.make_async_copy(k_ref.at[pl.ds(g * quarter, quarter)], k_own, local.at[1])
+    load_k.start()
+
+    def four(group):
+        return pl.ds(group * quarter, quarter)
+
+    def two(group, h):
+        return pl.ds(group * quarter + h * half_quarter, half_quarter)
+
+    def source(b, rel):
+        return c_ref if (b, rel) == (0, 0) else src.at[b, rel]
+
+    def turn(rel):
+        for t in range(quarter):
+            blocks[0, rel, t] = source(0, rel)[g * quarter + t].T
+
+    for s in range(pc):
+        dom[0, 0, s] = dom_ref[pl.ds(s, 1), :]
+    turn(0)
+
+    def table(t, carry):
+        at_pair = g * quarter + t
+        ways = owner_ref.shape[0]
+        named = [owner_ref[k, at_pair] for k in range(ways)]
+        slots = [slot_ref[k, at_pair] for k in range(ways)]
+        focks = [fock_ref[k, at_pair] for k in range(ways)]
+        for owner in range(n):
+            place, weight = 0, 0.0
+            for k in range(ways):
+                hit = named[k] == owner
+                place = jnp.where(hit, slots[k], place)
+                weight = jnp.where(hit, focks[k], weight)
+            bslot[0, t, owner] = place
+            bfock[0, t, owner] = weight
+        return carry
+
+    kinds = {
+        "slot": lambda b: bslot.at[b],
+        "fock": lambda b: bfock.at[b],
+        "dom": lambda b: bdom.at[b],
+    }
+    for rel in range(2):
+        kinds[rel] = functools.partial(lambda rel, b: blocks.at[b, rel], rel)
+    for rel in range(2, 4):
+        for h in (0, 1):
+            kinds[rel, h] = functools.partial(
+                lambda rel, h, b: blocks.at[b, rel, pl.ds(h * half_quarter, half_quarter)], rel, h
+            )
+
+    def ready(kind):
+        at_slot = kinds[kind]
+        ref = at_slot(0)
+        wires.start_all(end, [
+            (("far", kind), ref, at_slot(3), to_far),
+            (("beside", kind), ref, at_slot(4), to_beside),
+        ])
+        wires.start_all(mid, [
+            (("partner", kind), ref, at_slot(1), to_partner),
+            (("cross", kind), ref, at_slot(2), to_cross),
+        ])
+
+    first, second = 2 * inner, 1 + 2 * inner
+
+    def got_first(kind):
+        landed, passed = kinds[kind](2), kinds[kind](4)
+
+        def relay():
+            wires.wait(("cross", kind), landed)
+            wires.start_in(mid, ("beside", kind), landed, passed, to_beside)
+
+        pl.when(mid)(relay)
+
+    def got_second(kind):
+        at_slot = kinds[kind]
+        wires.wait(("partner", kind), at_slot(1), end)
+        wires.wait(("far", kind), at_slot(3), mid)
+        wires.start(("beside2", kind), at_slot(second), at_slot(5), to_beside)
+
+    def got_beside(kind):
+        wires.wait(("beside", kind), kinds[kind](4))
+
+    def got_beside2(kind):
+        wires.wait(("beside2", kind), kinds[kind](5))
+
+    places_of = (first, 4, second, 5)
+
+    lines = lax.broadcasted_iota(jnp.int32, (NB, rows), 0)
+    lines2 = lax.broadcasted_iota(jnp.int32, (2 * NB, 2 * rows), 0)
+
+    def expand(b, rel):
+        note("expand", b, rel)
+        base = groups[rel] * NB
+        block = source(b, rel)
+
+        def one(s, carry):
+            hit = (lines == (dom[b, rel, s] - base)).astype(F32).astype(BF16)
+            wide[b, s, pl.ds(rel * NB, NB)] = jnp.dot(
+                hit, block[s], preferred_element_type=F32
+            ).astype(BF16)
+            return carry
+
+        lax.fori_loop(0, pc, one, 0, unroll=4)
+
+    def make_turned(b, hs=(0, 1)):
+        note("make_turned", b)
+        place = places_of[b]
+
+        def one(t, carry):
+            for h in hs:
+                u, v = 2 * h, 2 * h + 1
+                row = jnp.concatenate(
+                    [
+                        bdom[place, u * quarter + t] - groups[u] * NB,
+                        bdom[place, v * quarter + t] - groups[v] * NB + NB,
+                    ],
+                    axis=1,
+                )
+                hit = (lines2 == row).astype(F32).astype(BF16)
+                both = jnp.concatenate([blocks[place, u, t], blocks[place, v, t]], axis=1)
+                turned[b, t, :, pl.ds(h * 2 * NB, 2 * NB)] = lax.dot_general(
+                    both, hit, (((1,), (1,)), ((), ())), preferred_element_type=F32
+                ).astype(BF16)
+            return carry
+
+        lax.fori_loop(0, quarter, one, 0, unroll=2)
+
+    owners = (p, partner)
+
+    def make_x(b, s):
+        note("make_x", b, s)
+        place = places_of[b]
+
+        def one(t, carry):
+            at_source = bslot[place, t, owners[s]]
+            x[b, t, s] = jnp.dot(
+                turned[b, t], wide[s, at_source], preferred_element_type=F32
+            ).astype(BF16)
+            return carry
+
+        lax.fori_loop(0, quarter, one, 0, unroll=4)
+
+    def couple(b, s, it):
+        note("couple", b, s)
+        place = places_of[b]
+        found = []
+        for t in range(quarter):
+            at_source = bslot[place, t, owners[s]]
+            xs = x[b, t, s]
+            half = jnp.dot(xs, amps[it][s][at_source], preferred_element_type=F32).astype(BF16)
+            found.append((t, xs, half))
+        for t, xs, half in found:
+            y = lax.dot_general(half, xs, (((1,), (1,)), ((), ())), preferred_element_type=F32)
+            y = bfock[place, t, owners[s]] * y
+            if s == 0:
+                acc[b, t] = y
+            elif b % 2 == 0:
+                acc[b, t] += y
+            else:
+                yout[it, b // 2, t] = (acc[b, t] + y).astype(BF16)
+
+    def post(it, m):
+        for t in range(quarter):
+            wires.start(("y", it, m, t), yout.at[it, m, t], yx.at[it, m, t], to_beside)
+
+    def share_partner(it, h):
+        part = two(g, h)
+        wires.start(("a", it, 0, h), amps[it][0].at[part], amps[it][1].at[part], to_partner)
+
+    def pass_partner(it, h):
+        part = two(g, h)
+        wires.wait(("a", it, 0, h), amps[it][1].at[part])
+        for key, peer in ((1, to_across), (2, to_mate)):
+            wires.start(("a", it, key, h), amps[it][1].at[part], amps[it][1].at[part], peer)
+
+    def pass_across(it, h):
+        part = two(across, h)
+        wires.wait(("a", it, 1, h), amps[it][1].at[part])
+        wires.start(("a", it, 3, h), amps[it][1].at[part], amps[it][1].at[part], to_mate)
+
+    def have_partner(it):
+        for h in (0, 1):
+            wires.wait(("a", it, 2, h), amps[it][1].at[two(mate, h)])
+            wires.wait(("a", it, 3, h), amps[it][1].at[two(diagonal, h)])
+
+    def sum_second(it):
+        for t in range(quarter):
+            wires.wait(("y", it, 1, t), yx.at[it, 1, t])
+            ysum[it, 1, t] = (acc[2, t] + yx[it, 1, t].astype(F32)).astype(BF16)
+            wires.start_all(end, [(("yend", it, t), ysum.at[it, 1, t], yin.at[it, 0, t], to_partner)])
+            wires.start_all(mid, [(("yfar", it, t), ysum.at[it, 1, t], yin.at[it, 0, t], to_far)])
+
+    def sum_first(it):
+        for t in range(quarter):
+            wires.wait(("y", it, 0, t), yx.at[it, 0, t])
+            total = acc[0, t] + yx[it, 0, t].astype(F32)
+            acc[0, t] = total
+            ysum[it, 0, t] = total.astype(BF16)
+            wires.start_all(mid, [(("ynear", it, t), ysum.at[it, 0, t], yin.at[it, 1, t], to_cross)])
+
+    def updated(it, t):
+        wires.wait(("ynear", it, t), yin.at[it, 1, t], mid)
+        wires.wait(("yend", it, t), yin.at[it, 0, t], mid)
+        wires.wait(("yfar", it, t), yin.at[it, 0, t], end)
+        at_pair = g * quarter + t
+        near = yin[it, 1, t].astype(F32)
+        total = yin[it, 0, t].astype(F32) + jnp.where(mid, near, acc[0, t])
+        row = jnp.broadcast_to(e_ref[pl.ds(at_pair, 1), :], (width, width))
+        return (-(k_own[t] + total) / (row.T + row + shift_ref[at_pair])).astype(BF16)
+
+    swap_mate, swap_across = (1, 0, 3, 2), (2, 3, 0, 1)
+
+    def from_mate(i):
+        part = four(groups[i])
+        wires.wait(("own mate", swap_mate[i]), src.at[0, 1, part])
+
+    def from_across(i):
+        part = four(groups[i])
+        wires.wait(("own across", swap_across[i]), src.at[0, 2, part])
+        wires.start(("own corner", i), src.at[0, 2, part], src.at[0, 3, part], to_mate)
+
+    def from_corner(i):
+        part = four(groups[i])
+        wires.wait(("own corner", swap_mate[i]), src.at[0, 3, part])
+
+    def to_next(i):
+        part = four(groups[i])
+        wires.start(("next", i), c_ref.at[part], src.at[1, 0, part], to_partner)
+
+    def from_next(i):
+        part = four(groups[i])
+        wires.wait(("next", i), src.at[1, 0, part])
+        wires.start(("next across", i), src.at[1, 0, part], src.at[1, 2, part], to_across)
+        wires.start(("next mate", i), src.at[1, 0, part], src.at[1, 1, part], to_mate)
+
+    def from_next_across(i):
+        part = four(groups[i])
+        wires.wait(("next across", swap_across[i]), src.at[1, 2, part])
+        wires.start(("next corner", i), src.at[1, 2, part], src.at[1, 3, part], to_mate)
+
+    def from_next_mate(i):
+        wires.wait(("next mate", swap_mate[i]), src.at[1, 1, four(groups[i])])
+
+    def from_next_corner(i):
+        wires.wait(("next corner", swap_mate[i]), src.at[1, 3, four(groups[i])])
+
+    def cast(s, carry):
+        amps[0][0][s] = start[s].astype(BF16)
+        return carry
+
+    small = ("slot", "fock", "dom")
+    late = ((2, 0), (2, 1), (3, 0), (3, 1))
+
+    pl.semaphore_wait(barrier, 5 + inner)
+    wires.start(("d", 1), dom.at[0, 0], dom.at[0, 1], to_mate)
+    wires.start(("d", 2), dom.at[0, 0], dom.at[0, 2], to_across)
+    for i in (2, 3, 0, 1):
+        part = four(groups[i])
+        wires.start(("own across", i), c_ref.at[part], src.at[0, 2, part], to_across)
+    ready(0)
+    for i in (1, 0, 2, 3):
+        part = four(groups[i])
+        wires.start(("own mate", i), c_ref.at[part], src.at[0, 1, part], to_mate)
+    from_mate(0)
+    turn(1)
+    ready(1)
+    to_next(0)
+    to_next(1)
+    lax.fori_loop(0, quarter, table, 0)
+    wires.wait(("d", 1), dom.at[0, 1])
+    wires.wait(("d", 2), dom.at[0, 2])
+    wires.start(("d", 3), dom.at[0, 2], dom.at[0, 3], to_mate)
+    load_start.wait()
+    lax.fori_loop(0, pc, cast, 0, unroll=2)
+    wires.wait(("d", 3), dom.at[0, 3])
+    for rel in range(4):
+        for t in range(quarter):
+            bdom[0, rel * quarter + t] = dom[0, rel, g * quarter + t]
+    wires.start(("d", 4), dom.at[0], dom.at[1], to_partner)
+    for kind in small:
+        ready(kind)
+    from_across(0)
+    turn(2)
+    got_first(0)
+    got_second(0)
+    expand(0, 0)
+    from_across(1)
+    from_corner(0)
+    turn(3)
+    to_next(2)
+    share_partner(0, 0)
+    share_partner(0, 1)
+    to_next(3)
+    for kind in late:
+        ready(kind)
+    got_first(1)
+    got_second(1)
+    from_across(2)
+    from_next(0)
+    for i in (1, 2, 3):
+        from_mate(i)
+    expand(0, 1)
+    from_across(3)
+    from_next(1)
+    for kind in small:
+        got_first(kind)
+    for i in (1, 2, 3):
+        from_corner(i)
+    from_next_across(2)
+    for kind in late:
+        got_first(kind)
+    expand(0, 2)
+    from_next(2)
+    expand(0, 3)
+    for h in (0, 1):
+        pass_partner(0, h)
+    from_next_across(3)
+    wires.wait(("d", 4), dom.at[1])
+    from_next(3)
+    for kind in small:
+        got_second(kind)
+    for i in range(4):
+        from_next_mate(i)
+    expand(1, 0)
+    from_next_across(0)
+    make_turned(0)
+    make_x(0, 0)
+    for kind in ((2, 0), (2, 1)):
+        got_second(kind)
+    pass_across(0, 0)
+    pass_across(0, 1)
+    for kind in (*small, 0, 1, *late):
+        got_beside(kind)
+    make_turned(1)
+    make_x(1, 0)
+    for kind in ((3, 0),):
+        got_second(kind)
+    from_next_across(1)
+    for kind in ((3, 1),):
+        got_second(kind)
+    expand(1, 1)
+    have_partner(0)
+    for i in range(4):
+        from_next_corner(i)
+    expand(1, 2)
+    expand(1, 3)
+    make_x(1, 1)
+    couple(1, 0, 0)
+    couple(1, 1, 0)
+    post(0, 0)
+    make_turned(2)
+    make_x(2, 0)
+    make_x(2, 1)
+    couple(2, 0, 0)
+    couple(2, 1, 0)
+    make_x(0, 1)
+    for kind in (*small, 0, 1, *late):
+        got_beside2(kind)
+    make_turned(3)
+    make_x(3, 0)
+    make_x(3, 1)
+    couple(3, 0, 0)
+    couple(3, 1, 0)
+    post(0, 1)
+    couple(0, 0, 0)
+    couple(0, 1, 0)
+    load_k.wait()
+    sum_first(0)
+    sum_second(0)
+
+    for t in range(quarter):
+        amps[1][0][g * quarter + t] = updated(0, t)
+        if t % half_quarter == half_quarter - 1:
+            h = t // half_quarter
+            part = two(g, h)
+            share_partner(1, h)
+            wires.start(("own", 1, h), amps[1][0].at[part], amps[1][0].at[part], to_across)
+            wires.start(("own", 2, h), amps[1][0].at[part], amps[1][0].at[part], to_mate)
+    for h in (0, 1):
+        pass_partner(1, h)
+        part = two(across, h)
+        wires.wait(("own", 1, h), amps[1][0].at[part])
+        wires.start(("own", 3, h), amps[1][0].at[part], amps[1][0].at[part], to_mate)
+    for h in (0, 1):
+        wires.wait(("own", 2, h), amps[1][0].at[two(mate, h)])
+        wires.wait(("own", 3, h), amps[1][0].at[two(diagonal, h)])
+    couple(3, 0, 1)
+    couple(1, 0, 1)
+    pass_across(1, 0)
+    couple(2, 0, 1)
+    pass_across(1, 1)
+    couple(0, 0, 1)
+    have_partner(1)
+    couple(3, 1, 1)
+    post(1, 1)
+    couple(1, 1, 1)
+    post(1, 0)
+    couple(2, 1, 1)
+    couple(0, 1, 1)
+    sum_second(1)
+    sum_first(1)
+
+    for t in range(quarter):
+        value = updated(1, t)
+        mine[t] = value
+        out_ref[g * quarter + t] = value
+        if t % half_quarter == half_quarter - 1:
+            h = t // half_quarter
+            part = pl.ds(h * half_quarter, half_quarter)
+            wires.start(("out", 1, h), mine.at[part], out_ref.at[two(g, h)], to_across)
+            wires.start(("out", 2, h), mine.at[part], out_ref.at[two(g, h)], to_mate)
+    for h in (0, 1):
+        part = out_ref.at[two(across, h)]
+        wires.wait(("out", 1, h), part)
+        wires.start(("out", 3, h), part, part, to_mate)
+    for h in (0, 1):
+        wires.wait(("out", 2, h), out_ref.at[two(mate, h)])
+        wires.wait(("out", 3, h), out_ref.at[two(diagonal, h)])
+    wires.drain()
+
+
+WIRES = 190
+
+
+def quadrants_fit(n, groups, pc):
+    return n == 2 * groups and groups == 4 and pc % (2 * groups) == 0
+
+
+def quadrants_kernel(n, *refs):
+    quadrants(n, *refs)
+
+
+def quadrants_call(
+    n, owner, slot, fock, shift, coefficients, domain, start, integrals, energy
+):
+    pc, rows, width = coefficients.shape
+    quarter = pc // 4
+    big = (width, width)
+    vmem, smem = pl.BlockSpec(memory_space=pltpu.VMEM), pl.BlockSpec(memory_space=pltpu.SMEM)
+    hbm = pl.BlockSpec(memory_space=pl.ANY)
+    dma = pltpu.SemaphoreType.DMA
+    return pl.pallas_call(
+        functools.partial(quadrants_kernel, n),
+        out_shape=jax.ShapeDtypeStruct((pc, *big), BF16),
+        in_specs=[smem, smem, smem, smem, vmem, vmem, hbm, hbm, vmem],
+        out_specs=vmem,
+        scratch_shapes=[
+            pltpu.VMEM((2, 4, pc, rows, width), BF16),
+            pltpu.VMEM((2, 4, pc, 1, rows), jnp.int32),
+            pltpu.VMEM((6, 4, quarter, width, rows), BF16),
+            pltpu.VMEM((6, 4 * quarter, 1, rows), jnp.int32),
+            pltpu.SMEM((6, quarter, n), jnp.int32),
+            pltpu.SMEM((6, quarter, n), F32),
+            pltpu.VMEM((2, pc, 4 * NB, width), BF16),
+            pltpu.VMEM((4, quarter, width, 4 * NB), BF16),
+            pltpu.VMEM((4, quarter, 2, *big), BF16),
+            pltpu.VMEM((pc, *big), F32),
+            pltpu.VMEM((quarter, *big), F32),
+            *[pltpu.VMEM((pc, *big), BF16)] * 4,
+            pltpu.VMEM((4, quarter, *big), F32),
+            pltpu.VMEM((2, 2, quarter, *big), BF16),
+            pltpu.VMEM((2, 2, quarter, *big), BF16),
+            pltpu.VMEM((2, 2, quarter, *big), BF16),
+            pltpu.VMEM((2, 2, quarter, *big), BF16),
+            pltpu.VMEM((quarter, *big), BF16),
+            dma((WIRES,)), dma((WIRES,)), dma((2,)),
+        ],
+        compiler_params=pltpu.CompilerParams(
+            collective_id=0, has_side_effects=True, vmem_limit_bytes=60 * 2**20
+        ),
+        name="quadrants",
+    )(owner.T, slot.T, fock.T, shift, coefficients, domain, start, integrals, energy).astype(F32)
+
+
 def on_device(
     coefficients, domain, coupling_owner, coupling_slot, coupling_fock,
     exchange_integrals, pno_energy, pair_shift, amplitudes_start,
@@ -502,6 +1060,12 @@
     def params(collective):
         return pltpu.CompilerParams(
             collective_id=collective, has_side_effects=True, vmem_limit_bytes=60 * 2**20
+        )
+
+    if quadrants_fit(n, lax.axis_size("grp"), pc):
+        return quadrants_call(
+            n, coupling_owner, coupling_slot, coupling_fock, pair_shift, coefficients, domain,
+            amplitudes_start, exchange_integrals, pno_energy,
         )
 
     big = (width, width)

time: 112 us -> 81.6 us (0.73)
  Pallas kernels: 107 us -> 78.3 us
  local copies, waits for them, and re-layouts: 1.42 us -> 0 us
  other arithmetic: 3.52 us -> 2.12 us
    pallas_call x1, Pallas kernels: 107 us -> 78.3 us  [quadrants_call(): pl.pallas_call(functools.partial(quadrants_kernel, n), out_shape=jax.Shap...]
where the time goes in v1:
time: 81.6 us; the launch traced here: 80.5 us
  Pallas kernels  78.3 us (96%)
  other arithmetic  2.12 us (3%)
    pallas_call x1, Pallas kernels, quadrants_call(): pl.pallas_call(functools.partial(quadrants_kernel, n), out_shape=jax.Shap...  78.3 us
    convert_element_type x1, other arithmetic, quadrants_call(): return pl.pallas_call(functools.partial(quadrants_kernel, n), out_shape=j...  2.12 us

profile of v1, /device:TPU:0, one launch (start us, length us, event | category | flops | bytes accessed | tf_op | source)
XLA Modules:
  0.0 80.5 jit_solution(8692591667425542566)
XLA Ops:
  0.0 78.3 %quadrants.1 = bf16[16,128,128]{2,1,0:T(8,128)(2,1)} custom-call(s32[8,16]{1,0:T(8,128)} %bitcast.3, s32[8,16]{1,0:T(8,128)} %bitcast.4, f32[8,16]{1,0:T(8,128)} %bitcast.5, f32[16]{0:T(128)} %refs_3_.1, bf16[16,128,128]{2,1,0:T(8,128)(2,1)} %refs_4_.1, s32[16,128]{1,0:T(8,128)} %refs_5_.1, f32[16,128,128]{2,1,0:T(8,128)} %refs_6_.1, ...), custom_call_target="tpu_custom_call" | custom-call | tf_op jit(solution)/shard_map/quadrants/pallas_call | solution.py:1012
  78.3 2.1 %convert_element_type.3 = f32[16,128,128]{2,1,0:T(8,128)} convert(bf16[16,128,128]{2,1,0:T(8,128)(2,1)} %quadrants.1) | non-fusion elementwise | flops 262144 | bytes 1572864 | tf_op jit(solution)/shard_map/convert_element_type | solution.py:1042

commit v2 on v1

--- a/solution.py
+++ b/solution.py
@@ -487,42 +487,48 @@
 class Wires:
     def __init__(self, send, recv, here):
         self.send, self.recv, self.here = send, recv, here
-        self.ids, self.started = {}, []
-
-    def link(self, key, src, dst, peer):
-        at_key = self.ids.setdefault(key, len(self.ids))
-        return remote(src, dst, self.send.at[at_key], self.recv.at[at_key], peer)
-
-    def start(self, key, src, dst, peer, when=None):
-        copy = self.link(key, src, dst, peer)
+        self.sends, self.recvs, self.wholes = {}, {}, {}
+
+    def link(self, key, src, dst, peer, out=None):
+        out = key if out is None else out
+        at_send = self.sends.setdefault(out, len(self.sends))
+        at_recv = self.recvs.setdefault(key, len(self.recvs))
+        return remote(src, dst, self.send.at[at_send], self.recv.at[at_recv], peer)
+
+    def start_in(self, when, key, src, dst, peer, out=None, whole=None):
+        self.link(key, src, dst, peer, out).start()
+        out = key if out is None else out
+        role = 0 if when is None else 1 + (when is self.mid)
+        self.wholes[out, role] = (src if whole is None else whole, when)
+
+    def start(self, key, src, dst, peer, when=None, out=None, whole=None):
+        def run():
+            self.start_in(when, key, src, dst, peer, out, whole)
+
         if when is None:
-            copy.start()
+            run()
         else:
-            pl.when(when)(copy.start)
-        self.started.append((key, src, dst, peer, when))
-
-    def start_in(self, when, key, src, dst, peer):
-        copy = self.link(key, src, dst, peer)
-        copy.start()
-        self.started.append((key, src, dst, peer, when))
+            pl.when(when)(run)
 
     def start_all(self, when, jobs):
         def run():
-            for key, src, dst, peer in jobs:
-                self.start_in(when, key, src, dst, peer)
+            for job in jobs:
+                self.start_in(when, *job)
 
         pl.when(when)(run)
 
     def wait(self, key, dst, when=None):
-        copy = self.link(key, dst, dst, self.here)
+        at_recv = self.recvs.setdefault(key, len(self.recvs))
+        copy = remote(dst, dst, self.send.at[0], self.recv.at[at_recv], self.here)
         if when is None:
             copy.wait_recv()
         else:
             pl.when(when)(copy.wait_recv)
 
     def drain(self):
-        for *what, when in self.started:
-            copy = self.link(*what)
+        for (out, _), (whole, when) in self.wholes.items():
+            at_send = self.sends[out]
+            copy = remote(whole, whole, self.send.at[at_send], self.recv.at[0], self.here)
             if when is None:
                 copy.wait_send()
             else:
@@ -534,9 +540,9 @@
 
 
 def quadrants(
-    n, owner_ref, slot_ref, fock_ref, shift_ref, c_ref, dom_ref, start_ref, k_ref, e_ref, out_ref,
-    src, dom, blocks, bdom, bslot, bfock, wide, turned, x, start, k_own, amps_a, amps_b, amps_c, amps_d,
-    acc, yout, yx, ysum, yin, mine, send, recv, local,
+    n, owner_hbm, slot_hbm, fock_hbm, shift_hbm, c_hbm, dom_hbm, start_ref, k_ref, e_hbm, out_ref,
+    owner_ref, slot_ref, fock_ref, shift_ref, c_ref, dom_ref, e_ref, src, dom, blocks, bdom, bslot, bfock, wide, turned, x, start, k_own, amps_a, amps_b, amps_c, amps_d,
+    acc, yout, yx, ysum, yin, mine, send, recv, local, nearby,
 ):
     p, g = lax.axis_index("pairs"), lax.axis_index("grp")
     pc, rows, width = c_ref.shape
@@ -563,20 +569,33 @@
     def hello(peer):
         pl.semaphore_signal(barrier, inc=1, device_id=peer, device_id_type=MESH)
 
-    for peer in (to_far, to_partner, to_beside, to_across, to_mate):
+    for peer in (to_partner, to_beside, to_across, to_mate):
         hello(peer)
     pl.when(mid)(lambda: hello(to_cross))
 
-    load_start = pltpu.make_async_copy(start_ref, start, local.at[0])
-    load_start.start()
-    load_k = pltpu.make_async_copy(k_ref.at[pl.ds(g * quarter, quarter)], k_own, local.at[1])
-    load_k.start()
+    pairs = (
+        (c_hbm, c_ref), (dom_hbm, dom_ref), (owner_hbm, owner_ref), (slot_hbm, slot_ref),
+        (fock_hbm, fock_ref), (shift_hbm, shift_ref), (e_hbm, e_ref), (start_ref, start),
+        (k_ref.at[pl.ds(g * quarter, quarter)], k_own),
+    )
+    loads = [pltpu.make_async_copy(*pair, local.at[i]) for i, pair in enumerate(pairs)]
+    for load in loads:
+        load.start()
+    load_c, load_dom, load_owner, load_slot, load_fock, load_shift, load_e, load_start, load_k = loads
+    load_c.wait()
+    load_dom.wait()
 
     def four(group):
         return pl.ds(group * quarter, quarter)
 
     def two(group, h):
         return pl.ds(group * quarter + h * half_quarter, half_quarter)
+
+    def both_quarters(ref):
+        return ref.at[pl.ds(0, 2 * quarter)]
+
+    def three_quarters(ref):
+        return ref.at[pl.ds(0, 3 * quarter)]
 
     def source(b, rel):
         return c_ref if (b, rel) == (0, 0) else src.at[b, rel]
@@ -605,6 +624,7 @@
             bfock[0, t, owner] = weight
         return carry
 
+    small = ("slot", "fock", "dom")
     kinds = {
         "slot": lambda b: bslot.at[b],
         "fock": lambda b: bfock.at[b],
@@ -621,37 +641,47 @@
     def ready(kind):
         at_slot = kinds[kind]
         ref = at_slot(0)
+        whole, tag = (ref, kind) if kind in small else (blocks.at[0], 0)
+        together = ("beside", tag)
         wires.start_all(end, [
-            (("far", kind), ref, at_slot(3), to_far),
-            (("beside", kind), ref, at_slot(4), to_beside),
+            (("second", kind), ref, at_slot(3), to_far, ("second", tag), whole),
+            (together, ref, at_slot(4), to_beside, together, whole),
         ])
         wires.start_all(mid, [
-            (("partner", kind), ref, at_slot(1), to_partner),
-            (("cross", kind), ref, at_slot(2), to_cross),
+            (("second", kind), ref, at_slot(1), to_partner, ("second", tag), whole),
+            (("cross", kind), ref, at_slot(2), to_cross, ("cross", tag), whole),
         ])
 
     first, second = 2 * inner, 1 + 2 * inner
 
     def got_first(kind):
         landed, passed = kinds[kind](2), kinds[kind](4)
+        whole, tag = (landed, kind) if kind in small else (blocks.at[2], 0)
+        together = ("beside", tag)
 
         def relay():
             wires.wait(("cross", kind), landed)
-            wires.start_in(mid, ("beside", kind), landed, passed, to_beside)
+            wires.start_in(mid, together, landed, passed, to_beside, together, whole)
 
         pl.when(mid)(relay)
 
     def got_second(kind):
         at_slot = kinds[kind]
-        wires.wait(("partner", kind), at_slot(1), end)
-        wires.wait(("far", kind), at_slot(3), mid)
-        wires.start(("beside2", kind), at_slot(second), at_slot(5), to_beside)
-
-    def got_beside(kind):
-        wires.wait(("beside", kind), kinds[kind](4))
-
-    def got_beside2(kind):
-        wires.wait(("beside2", kind), kinds[kind](5))
+        landed = at_slot(second)
+        whole, tag = (landed, kind) if kind in small else (blocks.at[0], 0)
+        together = ("beside2", tag)
+        wires.wait(("second", kind), landed)
+        wires.start(together, landed, at_slot(5), to_beside, None, together, whole)
+
+    def got_beside():
+        for kind in small:
+            wires.wait(("beside", kind), kinds[kind](4))
+        wires.wait(("beside", 0), blocks.at[4])
+
+    def got_beside2():
+        for kind in small:
+            wires.wait(("beside2", kind), kinds[kind](5))
+        wires.wait(("beside2", 0), blocks.at[5])
 
     places_of = (first, 4, second, 5)
 
@@ -731,34 +761,42 @@
 
     def post(it, m):
         for t in range(quarter):
-            wires.start(("y", it, m, t), yout.at[it, m, t], yx.at[it, m, t], to_beside)
+            wires.start(
+                ("y", it, m, t), yout.at[it, m, t], yx.at[it, m, t], to_beside, None,
+                ("y", it, m), yout.at[it, m],
+            )
 
     def share_partner(it, h):
         part = two(g, h)
-        wires.start(("a", it, 0, h), amps[it][0].at[part], amps[it][1].at[part], to_partner)
+        wires.start(
+            ("a", it, 0, h), amps[it][0].at[part], amps[it][1].at[part], to_partner, None,
+            ("a", it, 0), amps[it][0].at[four(g)],
+        )
 
     def pass_partner(it, h):
         part = two(g, h)
         wires.wait(("a", it, 0, h), amps[it][1].at[part])
-        for key, peer in ((1, to_across), (2, to_mate)):
-            wires.start(("a", it, key, h), amps[it][1].at[part], amps[it][1].at[part], peer)
+        ref = amps[it][1].at[part]
+        wires.start(("a", it, 1, h), ref, ref, to_across, None, ("a", it, 1), amps[it][1].at[four(g)])
+        wires.start(("a", it, 2), ref, ref, to_mate, None, ("a", it, 2), both_quarters(amps[it][1]))
 
     def pass_across(it, h):
         part = two(across, h)
         wires.wait(("a", it, 1, h), amps[it][1].at[part])
-        wires.start(("a", it, 3, h), amps[it][1].at[part], amps[it][1].at[part], to_mate)
+        ref = amps[it][1].at[part]
+        wires.start(("a", it, 2), ref, ref, to_mate, None, ("a", it, 2), both_quarters(amps[it][1]))
 
     def have_partner(it):
-        for h in (0, 1):
-            wires.wait(("a", it, 2, h), amps[it][1].at[two(mate, h)])
-            wires.wait(("a", it, 3, h), amps[it][1].at[two(diagonal, h)])
+        wires.wait(("a", it, 2), both_quarters(amps[it][1]))
 
     def sum_second(it):
         for t in range(quarter):
             wires.wait(("y", it, 1, t), yx.at[it, 1, t])
             ysum[it, 1, t] = (acc[2, t] + yx[it, 1, t].astype(F32)).astype(BF16)
-            wires.start_all(end, [(("yend", it, t), ysum.at[it, 1, t], yin.at[it, 0, t], to_partner)])
-            wires.start_all(mid, [(("yfar", it, t), ysum.at[it, 1, t], yin.at[it, 0, t], to_far)])
+            job = (("yfar", it, t), ysum.at[it, 1, t], yin.at[it, 0, t])
+            group = (("yfar", it), ysum.at[it, 1])
+            wires.start_all(end, [(*job, to_partner, *group)])
+            wires.start_all(mid, [(*job, to_far, *group)])
 
     def sum_first(it):
         for t in range(quarter):
@@ -766,76 +804,113 @@
             total = acc[0, t] + yx[it, 0, t].astype(F32)
             acc[0, t] = total
             ysum[it, 0, t] = total.astype(BF16)
-            wires.start_all(mid, [(("ynear", it, t), ysum.at[it, 0, t], yin.at[it, 1, t], to_cross)])
+            wires.start_all(mid, [(
+                ("ynear", it, t), ysum.at[it, 0, t], yin.at[it, 1, t], to_cross,
+                ("ynear", it), ysum.at[it, 0],
+            )])
+
+    def coupled(it, t):
+        wires.wait(("ynear", it, t), yin.at[it, 1, t], mid)
+        wires.wait(("yfar", it, t), yin.at[it, 0, t])
+        near = yin[it, 1, t].astype(F32)
+        return yin[it, 0, t].astype(F32) + jnp.where(mid, near, acc[0, t])
 
     def updated(it, t):
-        wires.wait(("ynear", it, t), yin.at[it, 1, t], mid)
-        wires.wait(("yend", it, t), yin.at[it, 0, t], mid)
-        wires.wait(("yfar", it, t), yin.at[it, 0, t], end)
         at_pair = g * quarter + t
-        near = yin[it, 1, t].astype(F32)
-        total = yin[it, 0, t].astype(F32) + jnp.where(mid, near, acc[0, t])
+        total = coupled(it, t)
         row = jnp.broadcast_to(e_ref[pl.ds(at_pair, 1), :], (width, width))
         return (-(k_own[t] + total) / (row.T + row + shift_ref[at_pair])).astype(BF16)
 
     swap_mate, swap_across = (1, 0, 3, 2), (2, 3, 0, 1)
 
-    def from_mate(i):
-        part = four(groups[i])
-        wires.wait(("own mate", swap_mate[i]), src.at[0, 1, part])
+    def from_mate():
+        wires.wait(("own mate", 1), src.at[0, 1, four(g)])
+
+    def from_mate_rest():
+        wires.wait(("own mate", 0), three_quarters(src.at[0, 1]))
 
     def from_across(i):
         part = four(groups[i])
         wires.wait(("own across", swap_across[i]), src.at[0, 2, part])
-        wires.start(("own corner", i), src.at[0, 2, part], src.at[0, 3, part], to_mate)
-
-    def from_corner(i):
-        part = four(groups[i])
-        wires.wait(("own corner", swap_mate[i]), src.at[0, 3, part])
+        wires.start(
+            ("own corner", int(i == 1)), src.at[0, 2, part], src.at[0, 3, part], to_mate, None,
+            ("own corner", 0), src.at[0, 2],
+        )
+
+    def from_corner():
+        wires.wait(("own corner", 1), src.at[0, 3, four(g)])
+
+    def from_corner_rest():
+        wires.wait(("own corner", 0), three_quarters(src.at[0, 3]))
 
     def to_next(i):
         part = four(groups[i])
-        wires.start(("next", i), c_ref.at[part], src.at[1, 0, part], to_partner)
+        wires.start(
+            ("next", i), c_ref.at[part], src.at[1, 0, part], to_partner, None, ("next", 0), c_ref
+        )
 
     def from_next(i):
         part = four(groups[i])
         wires.wait(("next", i), src.at[1, 0, part])
-        wires.start(("next across", i), src.at[1, 0, part], src.at[1, 2, part], to_across)
-        wires.start(("next mate", i), src.at[1, 0, part], src.at[1, 1, part], to_mate)
+        ref = src.at[1, 0, part]
+        wires.start(
+            ("next across", i), ref, src.at[1, 2, part], to_across, None,
+            ("next across", 0), src.at[1, 0],
+        )
+        wires.start(
+            ("next mate", 0), ref, src.at[1, 1, part], to_mate, None,
+            ("next mate", 0), src.at[1, 0],
+        )
 
     def from_next_across(i):
         part = four(groups[i])
         wires.wait(("next across", swap_across[i]), src.at[1, 2, part])
-        wires.start(("next corner", i), src.at[1, 2, part], src.at[1, 3, part], to_mate)
-
-    def from_next_mate(i):
-        wires.wait(("next mate", swap_mate[i]), src.at[1, 1, four(groups[i])])
-
-    def from_next_corner(i):
-        wires.wait(("next corner", swap_mate[i]), src.at[1, 3, four(groups[i])])
+        wires.start(
+            ("next corner", 0), src.at[1, 2, part], src.at[1, 3, part], to_mate, None,
+            ("next corner", 0), src.at[1, 2],
+        )
+
+    def from_next_mate():
+        wires.wait(("next mate", 0), src.at[1, 1])
+
+    def from_next_corner():
+        wires.wait(("next corner", 0), src.at[1, 3])
 
     def cast(s, carry):
         amps[0][0][s] = start[s].astype(BF16)
         return carry
 
-    small = ("slot", "fock", "dom")
     late = ((2, 0), (2, 1), (3, 0), (3, 1))
 
-    pl.semaphore_wait(barrier, 5 + inner)
+    pl.semaphore_wait(barrier, 4 + inner)
+
+    def nearby_is_in():
+        pl.semaphore_signal(nearby, inc=1, device_id=to_partner, device_id_type=MESH)
+
+    pl.when(mid)(nearby_is_in)
     wires.start(("d", 1), dom.at[0, 0], dom.at[0, 1], to_mate)
     wires.start(("d", 2), dom.at[0, 0], dom.at[0, 2], to_across)
     for i in (2, 3, 0, 1):
         part = four(groups[i])
-        wires.start(("own across", i), c_ref.at[part], src.at[0, 2, part], to_across)
-    ready(0)
+        wires.start(
+            ("own across", i), c_ref.at[part], src.at[0, 2, part], to_across, None,
+            ("own across", 0), c_ref,
+        )
     for i in (1, 0, 2, 3):
         part = four(groups[i])
-        wires.start(("own mate", i), c_ref.at[part], src.at[0, 1, part], to_mate)
-    from_mate(0)
+        wires.start(
+            ("own mate", int(i == 1)), c_ref.at[part], src.at[0, 1, part], to_mate, None,
+            ("own mate", 0), c_ref,
+        )
+    pl.when(end)(lambda: pl.semaphore_wait(nearby, 1))
+    ready(0)
+    from_mate()
     turn(1)
     ready(1)
     to_next(0)
     to_next(1)
+    for load in (load_owner, load_slot, load_fock):
+        load.wait()
     lax.fori_loop(0, quarter, table, 0)
     wires.wait(("d", 1), dom.at[0, 1])
     wires.wait(("d", 2), dom.at[0, 2])
@@ -855,7 +930,7 @@
     got_second(0)
     expand(0, 0)
     from_across(1)
-    from_corner(0)
+    from_corner()
     turn(3)
     to_next(2)
     share_partner(0, 0)
@@ -867,15 +942,13 @@
     got_second(1)
     from_across(2)
     from_next(0)
-    for i in (1, 2, 3):
-        from_mate(i)
+    from_mate_rest()
     expand(0, 1)
     from_across(3)
     from_next(1)
     for kind in small:
         got_first(kind)
-    for i in (1, 2, 3):
-        from_corner(i)
+    from_corner_rest()
     from_next_across(2)
     for kind in late:
         got_first(kind)
@@ -889,8 +962,7 @@
     from_next(3)
     for kind in small:
         got_second(kind)
-    for i in range(4):
-        from_next_mate(i)
+    from_next_mate()
     expand(1, 0)
     from_next_across(0)
     make_turned(0)
@@ -899,8 +971,7 @@
         got_second(kind)
     pass_across(0, 0)
     pass_across(0, 1)
-    for kind in (*small, 0, 1, *late):
-        got_beside(kind)
+    got_beside()
     make_turned(1)
     make_x(1, 0)
     for kind in ((3, 0),):
@@ -910,8 +981,7 @@
         got_second(kind)
     expand(1, 1)
     have_partner(0)
-    for i in range(4):
-        from_next_corner(i)
+    from_next_corner()
     expand(1, 2)
     expand(1, 3)
     make_x(1, 1)
@@ -924,8 +994,7 @@
     couple(2, 0, 0)
     couple(2, 1, 0)
     make_x(0, 1)
-    for kind in (*small, 0, 1, *late):
-        got_beside2(kind)
+    got_beside2()
     make_turned(3)
     make_x(3, 0)
     make_x(3, 1)
@@ -934,7 +1003,8 @@
     post(0, 1)
     couple(0, 0, 0)
     couple(0, 1, 0)
-    load_k.wait()
+    for load in (load_k, load_e, load_shift):
+        load.wait()
     sum_first(0)
     sum_second(0)
 
@@ -943,17 +1013,21 @@
         if t % half_quarter == half_quarter - 1:
             h = t // half_quarter
             part = two(g, h)
+            ref = amps[1][0].at[part]
             share_partner(1, h)
-            wires.start(("own", 1, h), amps[1][0].at[part], amps[1][0].at[part], to_across)
-            wires.start(("own", 2, h), amps[1][0].at[part], amps[1][0].at[part], to_mate)
+            wires.start(
+                ("own", 1, h), ref, ref, to_across, None, ("own", 1), amps[1][0].at[four(g)]
+            )
+            wires.start(
+                ("own", 2), ref, ref, to_mate, None, ("own", 2), both_quarters(amps[1][0])
+            )
     for h in (0, 1):
         pass_partner(1, h)
         part = two(across, h)
         wires.wait(("own", 1, h), amps[1][0].at[part])
-        wires.start(("own", 3, h), amps[1][0].at[part], amps[1][0].at[part], to_mate)
-    for h in (0, 1):
-        wires.wait(("own", 2, h), amps[1][0].at[two(mate, h)])
-        wires.wait(("own", 3, h), amps[1][0].at[two(diagonal, h)])
+        ref = amps[1][0].at[part]
+        wires.start(("own", 2), ref, ref, to_mate, None, ("own", 2), both_quarters(amps[1][0]))
+    wires.wait(("own", 2), both_quarters(amps[1][0]))
     couple(3, 0, 1)
     couple(1, 0, 1)
     pass_across(1, 0)
@@ -971,25 +1045,25 @@
     sum_first(1)
 
     for t in range(quarter):
-        value = updated(1, t)
+        value = coupled(1, t).astype(BF16)
         mine[t] = value
         out_ref[g * quarter + t] = value
         if t % half_quarter == half_quarter - 1:
             h = t // half_quarter
-            part = pl.ds(h * half_quarter, half_quarter)
-            wires.start(("out", 1, h), mine.at[part], out_ref.at[two(g, h)], to_across)
-            wires.start(("out", 2, h), mine.at[part], out_ref.at[two(g, h)], to_mate)
+            part = mine.at[pl.ds(h * half_quarter, half_quarter)]
+            dst = out_ref.at[two(g, h)]
+            wires.start(("out", 1, h), part, dst, to_across, None, ("out", 1), mine)
+            wires.start(("out", 2), part, dst, to_mate, None, ("out", 2), both_quarters(out_ref))
     for h in (0, 1):
-        part = out_ref.at[two(across, h)]
-        wires.wait(("out", 1, h), part)
-        wires.start(("out", 3, h), part, part, to_mate)
-    for h in (0, 1):
-        wires.wait(("out", 2, h), out_ref.at[two(mate, h)])
-        wires.wait(("out", 3, h), out_ref.at[two(diagonal, h)])
+        ref = out_ref.at[two(across, h)]
+        wires.wait(("out", 1, h), ref)
+        wires.start(("out", 2), ref, ref, to_mate, None, ("out", 2), both_quarters(out_ref))
+    wires.wait(("out", 2), both_quarters(out_ref))
     wires.drain()
-
-
-WIRES = 190
+    assert len(wires.sends) <= SENDS and len(wires.recvs) <= RECVS, (len(wires.sends), len(wires.recvs))
+
+
+SENDS, RECVS = 45, 96
 
 
 def quadrants_fit(n, groups, pc):
@@ -1005,16 +1079,19 @@
 ):
     pc, rows, width = coefficients.shape
     quarter = pc // 4
-    big = (width, width)
-    vmem, smem = pl.BlockSpec(memory_space=pltpu.VMEM), pl.BlockSpec(memory_space=pltpu.SMEM)
-    hbm = pl.BlockSpec(memory_space=pl.ANY)
+    big, ways = (width, width), owner.shape[1]
+    vmem, hbm = pl.BlockSpec(memory_space=pltpu.VMEM), pl.BlockSpec(memory_space=pl.ANY)
     dma = pltpu.SemaphoreType.DMA
-    return pl.pallas_call(
+    total = pl.pallas_call(
         functools.partial(quadrants_kernel, n),
         out_shape=jax.ShapeDtypeStruct((pc, *big), BF16),
-        in_specs=[smem, smem, smem, smem, vmem, vmem, hbm, hbm, vmem],
+        in_specs=[hbm] * 9,
         out_specs=vmem,
         scratch_shapes=[
+            pltpu.SMEM((ways, pc), jnp.int32), pltpu.SMEM((ways, pc), jnp.int32),
+            pltpu.SMEM((ways, pc), F32), pltpu.SMEM((pc,), F32),
+            pltpu.VMEM((pc, rows, width), BF16), pltpu.VMEM((pc, rows), jnp.int32),
+            pltpu.VMEM((pc, width), F32),
             pltpu.VMEM((2, 4, pc, rows, width), BF16),
             pltpu.VMEM((2, 4, pc, 1, rows), jnp.int32),
             pltpu.VMEM((6, 4, quarter, width, rows), BF16),
@@ -1033,13 +1110,15 @@
             pltpu.VMEM((2, 2, quarter, *big), BF16),
             pltpu.VMEM((2, 2, quarter, *big), BF16),
             pltpu.VMEM((quarter, *big), BF16),
-            dma((WIRES,)), dma((WIRES,)), dma((2,)),
+            dma((SENDS,)), dma((RECVS,)), dma((9,)), pltpu.SemaphoreType.REGULAR,
         ],
         compiler_params=pltpu.CompilerParams(
             collective_id=0, has_side_effects=True, vmem_limit_bytes=60 * 2**20
         ),
         name="quadrants",
-    )(owner.T, slot.T, fock.T, shift, coefficients, domain, start, integrals, energy).astype(F32)
+    )(owner.T, slot.T, fock.T, shift, coefficients, domain, start, integrals, energy)
+    denominator = energy[:, :, None] + energy[:, None, :] + shift[:, None, None]
+    return -(integrals + total.astype(F32)) / denominator
 
 
 def on_device(

time: 81.6 us -> 78.2 us (0.958); the launches traced: 80.5 us -> 78 us
  Pallas kernels: 78.3 us -> 75.6 us
    pallas_call x1, Pallas kernels: 78.3 us -> 75.6 us  [quadrants_call(): pl.pallas_call(functools.partial(quadrants_kernel, n), out_shape=jax.Shap...]
    div x0 -> x1, other arithmetic: none -> 2.38 us  [quadrants_call(): return -(integrals + total.astype(F32)) / denominator]
    convert_element_type x1 -> x0, other arithmetic: 2.12 us -> none  [quadrants_call(): return pl.pallas_call(functools.partial(quadrants_kernel, n), out_shape=j...]
where the time goes in v2:
time: 78.2 us; the launch traced here: 78 us
  Pallas kernels  75.6 us (97%)
  other arithmetic  2.38 us (3%)
    pallas_call x1, Pallas kernels, quadrants_call(): pl.pallas_call(functools.partial(quadrants_kernel, n), out_shape=jax.Shap...  75.6 us
    div x1, other arithmetic, quadrants_call(): return -(integrals + total.astype(F32)) / denominator  2.38 us

profile of v2, /device:TPU:0, one launch (start us, length us, event | category | flops | bytes accessed | tf_op | source)
XLA Modules:
  0.0 78.0 jit_solution(11312107220899912443)
XLA Ops:
  0.0 0.0 copy-start
  0.0 0.0 copy-start.1
  0.0 0.0 copy-start.2
  0.0 75.6 %quadrants.1 = bf16[16,128,128]{2,1,0:T(8,128)(2,1)} custom-call(s32[8,16]{1,0:T(8,128)} %bitcast.3, s32[8,16]{1,0:T(8,128)} %bitcast.4, f32[8,16]{1,0:T(8,128)} %bitcast.5, f32[16]{0:T(128)} %refs_3_.1, bf16[16,128,128]{2,1,0:T(8,128)(2,1)} %refs_4_.1, s32[16,128]{1,0:T(8,128)} %refs_5_.1, f32[16,128,128]{2,1,0:T(8,128)} %refs_6_.1, ...), custom_call_target="tpu_custom_call" | custom-call | tf_op jit(solution)/shard_map/quadrants/pallas_call | solution.py:1085
  75.6 0.0 copy-done
  75.6 0.0 copy-done.1
  75.7 0.0 copy-done.2
  75.7 2.4 %add_divide_fusion = f32[16,128,128]{2,1,0:T(8,128)} fusion(f32[16,128,128]{2,1,0:T(8,128)S(1)} %copy-done, bf16[16,128,128]{2,1,0:T(8,128)(2,1)} %quadrants.1, f32[16]{0:T(128)S(1)} %copy-done.2, f32[16,128]{1,0:T(8,128)S(1)} %copy-done.1), kind=kLoop, calls=%fused_computation | loop fusion | flops 1572864 | bytes 2629696 | tf_op jit(solution)/shard_map/div | solution.py:1121
Async XLA Ops:
  0.0 75.6 %copy-start = (f32[16,128,128]{2,1,0:T(8,128)S(1)}, f32[16,128,128]{2,1,0:T(8,128)}, u32[]{:S(2)}) copy-start(f32[16,128,128]{2,1,0:T(8,128)} %refs_7_.1) | copy-start | bytes 3145732
  0.0 75.6 %copy-start.1 = (f32[16,128]{1,0:T(8,128)S(1)}, f32[16,128]{1,0:T(8,128)}, u32[]{:S(2)}) copy-start(f32[16,128]{1,0:T(8,128)} %refs_8_.1) | copy-start | bytes 24580
  0.0 75.7 %copy-start.2 = (f32[16]{0:T(128)S(1)}, f32[16]{0:T(128)}, u32[]{:S(2)}) copy-start(f32[16]{0:T(128)} %refs_3_.1) | copy-start | bytes 196

commit v3 on v2

--- a/solution.py
+++ b/solution.py
@@ -542,7 +542,7 @@
 def quadrants(
     n, owner_hbm, slot_hbm, fock_hbm, shift_hbm, c_hbm, dom_hbm, start_ref, k_ref, e_hbm, out_ref,
     owner_ref, slot_ref, fock_ref, shift_ref, c_ref, dom_ref, e_ref, src, dom, blocks, bdom, bslot, bfock, wide, turned, x, start, k_own, amps_a, amps_b, amps_c, amps_d,
-    acc, yout, yx, ysum, yin, mine, send, recv, local, nearby,
+    acc, yout, yx, ysum, yin, mine, send, recv, local,
 ):
     p, g = lax.axis_index("pairs"), lax.axis_index("grp")
     pc, rows, width = c_ref.shape
@@ -600,9 +600,9 @@
     def source(b, rel):
         return c_ref if (b, rel) == (0, 0) else src.at[b, rel]
 
-    def turn(rel):
+    def turn(rel, b=0):
         for t in range(quarter):
-            blocks[0, rel, t] = source(0, rel)[g * quarter + t].T
+            blocks[b, rel, t] = source(b, rel)[g * quarter + t].T
 
     for s in range(pc):
         dom[0, 0, s] = dom_ref[pl.ds(s, 1), :]
@@ -630,33 +630,43 @@
         "fock": lambda b: bfock.at[b],
         "dom": lambda b: bdom.at[b],
     }
-    for rel in range(2):
-        kinds[rel] = functools.partial(lambda rel, b: blocks.at[b, rel], rel)
-    for rel in range(2, 4):
+    for rel in range(4):
         for h in (0, 1):
             kinds[rel, h] = functools.partial(
                 lambda rel, h, b: blocks.at[b, rel, pl.ds(h * half_quarter, half_quarter)], rel, h
             )
+        kinds[rel] = functools.partial(lambda rel, b: blocks.at[b, rel], rel)
+
+    def grouped(kind, ref):
+        return (ref, kind) if kind in small else (blocks.at[0], 0)
 
     def ready(kind):
-        at_slot = kinds[kind]
-        ref = at_slot(0)
-        whole, tag = (ref, kind) if kind in small else (blocks.at[0], 0)
+        ref = kinds[kind](0)
+        whole, tag = grouped(kind, ref)
         together = ("beside", tag)
-        wires.start_all(end, [
-            (("second", kind), ref, at_slot(3), to_far, ("second", tag), whole),
-            (together, ref, at_slot(4), to_beside, together, whole),
-        ])
-        wires.start_all(mid, [
-            (("second", kind), ref, at_slot(1), to_partner, ("second", tag), whole),
-            (("cross", kind), ref, at_slot(2), to_cross, ("cross", tag), whole),
-        ])
+        if kind in ("slot", "fock"):
+            wires.start(("second", kind), ref, kinds[kind](1), to_partner)
+        wires.start_all(end, [(together, ref, kinds[kind](4), to_beside, together, whole)])
+        wires.start_all(
+            mid, [(("cross", kind), ref, kinds[kind](2), to_cross, ("cross", tag), whole)]
+        )
+
+    def next_ready(kind):
+        ref = kinds[kind](1)
+        whole, tag = grouped(kind, ref)
+        together = ("beside2", tag)
+        if kind in ("slot", "fock"):
+            wires.wait(("second", kind), ref)
+        wires.start_all(end, [(together, ref, kinds[kind](5), to_beside, together, whole)])
+        wires.start_all(
+            mid, [(("further", kind), ref, kinds[kind](3), to_cross, ("further", tag), whole)]
+        )
 
     first, second = 2 * inner, 1 + 2 * inner
 
     def got_first(kind):
         landed, passed = kinds[kind](2), kinds[kind](4)
-        whole, tag = (landed, kind) if kind in small else (blocks.at[2], 0)
+        whole, tag = grouped(kind, landed)
         together = ("beside", tag)
 
         def relay():
@@ -665,13 +675,16 @@
 
         pl.when(mid)(relay)
 
-    def got_second(kind):
-        at_slot = kinds[kind]
-        landed = at_slot(second)
-        whole, tag = (landed, kind) if kind in small else (blocks.at[0], 0)
+    def got_further(kind):
+        landed, passed = kinds[kind](3), kinds[kind](5)
+        whole, tag = grouped(kind, landed)
         together = ("beside2", tag)
-        wires.wait(("second", kind), landed)
-        wires.start(together, landed, at_slot(5), to_beside, None, together, whole)
+
+        def relay():
+            wires.wait(("further", kind), landed)
+            wires.start_in(mid, together, landed, passed, to_beside, together, whole)
+
+        pl.when(mid)(relay)
 
     def got_beside():
         for kind in small:
@@ -685,22 +698,32 @@
 
     places_of = (first, 4, second, 5)
 
-    lines = lax.broadcasted_iota(jnp.int32, (NB, rows), 0)
-    lines2 = lax.broadcasted_iota(jnp.int32, (2 * NB, 2 * rows), 0)
-
-    def expand(b, rel):
-        note("expand", b, rel)
+    lines = lax.broadcasted_iota(jnp.int16, (NB, rows), 0)
+    lines2 = lax.broadcasted_iota(jnp.int16, (2 * NB, 2 * rows), 0)
+
+    def one_hot(numbers, row):
+        hit = numbers == row.astype(jnp.int16)
+        return jnp.where(hit, jnp.ones(hit.shape, BF16), jnp.zeros(hit.shape, BF16))
+
+    def expand(b, rel, parts=(0, 1, 2, 3)):
         base = groups[rel] * NB
         block = source(b, rel)
 
         def one(s, carry):
-            hit = (lines == (dom[b, rel, s] - base)).astype(F32).astype(BF16)
+            hit = one_hot(lines, dom[b, rel, s] - base)
             wide[b, s, pl.ds(rel * NB, NB)] = jnp.dot(
                 hit, block[s], preferred_element_type=F32
             ).astype(BF16)
             return carry
 
-        lax.fori_loop(0, pc, one, 0, unroll=4)
+        if len(parts) == 4:
+            note("expand", b, rel)
+            lax.fori_loop(0, pc, one, 0, unroll=4)
+            return
+        for i in parts:
+            note("expand4", b, rel)
+            for t in range(quarter):
+                one(groups[i] * quarter + t, 0)
 
     def make_turned(b, hs=(0, 1)):
         note("make_turned", b)
@@ -716,7 +739,7 @@
                     ],
                     axis=1,
                 )
-                hit = (lines2 == row).astype(F32).astype(BF16)
+                hit = one_hot(lines2, row)
                 both = jnp.concatenate([blocks[place, u, t], blocks[place, v, t]], axis=1)
                 turned[b, t, :, pl.ds(h * 2 * NB, 2 * NB)] = lax.dot_general(
                     both, hit, (((1,), (1,)), ((), ())), preferred_element_type=F32
@@ -766,25 +789,40 @@
                 ("y", it, m), yout.at[it, m],
             )
 
-    def share_partner(it, h):
-        part = two(g, h)
+    def share(t):
+        at_pair = g * quarter + t
+        ref, part = amps[1][0].at[at_pair], amps[1][0].at[four(g)]
+        wires.start(("a", 1, 0, t), ref, amps[1][1].at[at_pair], to_partner, None, ("a", 1, 0), part)
+        wires.start(("own", 1, t), ref, ref, to_across, None, ("own", 1), part)
+        wires.start(("own", 2), ref, ref, to_mate, None, ("own", 2), both_quarters(amps[1][0]))
+
+    def pass_partner(t):
+        ref, part = amps[1][1].at[g * quarter + t], amps[1][1].at[four(g)]
+        wires.wait(("a", 1, 0, t), ref)
+        wires.start(("a", 1, 1, t), ref, ref, to_across, None, ("a", 1, 1), part)
+        wires.start(("a", 1, 2), ref, ref, to_mate, None, ("a", 1, 2), both_quarters(amps[1][1]))
+
+    def pass_own(t):
+        ref = amps[1][0].at[across * quarter + t]
+        wires.wait(("own", 1, t), ref)
+        wires.start(("own", 2), ref, ref, to_mate, None, ("own", 2), both_quarters(amps[1][0]))
+
+    def pass_across(t):
+        ref = amps[1][1].at[across * quarter + t]
+        wires.wait(("a", 1, 1, t), ref)
+        wires.start(("a", 1, 2), ref, ref, to_mate, None, ("a", 1, 2), both_quarters(amps[1][1]))
+
+    def share_start(j):
+        part = four((g, across)[j])
         wires.start(
-            ("a", it, 0, h), amps[it][0].at[part], amps[it][1].at[part], to_partner, None,
-            ("a", it, 0), amps[it][0].at[four(g)],
-        )
-
-    def pass_partner(it, h):
-        part = two(g, h)
-        wires.wait(("a", it, 0, h), amps[it][1].at[part])
-        ref = amps[it][1].at[part]
-        wires.start(("a", it, 1, h), ref, ref, to_across, None, ("a", it, 1), amps[it][1].at[four(g)])
-        wires.start(("a", it, 2), ref, ref, to_mate, None, ("a", it, 2), both_quarters(amps[it][1]))
-
-    def pass_across(it, h):
-        part = two(across, h)
-        wires.wait(("a", it, 1, h), amps[it][1].at[part])
-        ref = amps[it][1].at[part]
-        wires.start(("a", it, 2), ref, ref, to_mate, None, ("a", it, 2), both_quarters(amps[it][1]))
+            ("start", j), amps[0][0].at[part], amps[0][1].at[part], to_partner, None,
+            ("start", 0), both_quarters(amps[0][0]),
+        )
+
+    def pass_start(j):
+        ref = amps[0][1].at[four((g, across)[j])]
+        wires.wait(("start", j), ref)
+        wires.start(("a", 0, 2), ref, ref, to_mate, None, ("a", 0, 2), both_quarters(amps[0][1]))
 
     def have_partner(it):
         wires.wait(("a", it, 2), both_quarters(amps[it][1]))
@@ -851,140 +889,173 @@
 
     def from_next(i):
         part = four(groups[i])
-        wires.wait(("next", i), src.at[1, 0, part])
         ref = src.at[1, 0, part]
+        wires.wait(("next", i), ref)
+        if i in (2, 3):
+            wires.start(
+                ("next across", i), ref, src.at[1, 2, part], to_across, None,
+                ("next across", 0), both_quarters(src.at[1, 0]),
+            )
         wires.start(
-            ("next across", i), ref, src.at[1, 2, part], to_across, None,
-            ("next across", 0), src.at[1, 0],
-        )
+            ("next mate", int(i == 1)), ref, src.at[1, 1, part], to_mate, None,
+            ("next mate", 0), src.at[1, 0],
+        )
+
+    def to_wide(i):
+        part = four(groups[i])
         wires.start(
-            ("next mate", 0), ref, src.at[1, 1, part], to_mate, None,
-            ("next mate", 0), src.at[1, 0],
+            ("next wide", i), src.at[0, 2, part], src.at[1, 2, part], to_partner, None,
+            ("next wide", 0), both_quarters(src.at[0, 2]),
+        )
+
+    def corner(i):
+        part = four(groups[i])
+        wires.start(
+            ("next corner", int(i == 1)), src.at[1, 2, part], src.at[1, 3, part], to_mate, None,
+            ("next corner", 0), src.at[1, 2],
         )
 
     def from_next_across(i):
-        part = four(groups[i])
-        wires.wait(("next across", swap_across[i]), src.at[1, 2, part])
-        wires.start(
-            ("next corner", 0), src.at[1, 2, part], src.at[1, 3, part], to_mate, None,
-            ("next corner", 0), src.at[1, 2],
-        )
+        wires.wait(("next across", swap_across[i]), src.at[1, 2, four(groups[i])])
+        corner(i)
+
+    def from_wide(i):
+        wires.wait(("next wide", i), src.at[1, 2, four(groups[i])])
+        corner(i)
 
     def from_next_mate():
-        wires.wait(("next mate", 0), src.at[1, 1])
+        wires.wait(("next mate", 1), src.at[1, 1, four(g)])
+
+    def from_next_mate_rest():
+        wires.wait(("next mate", 0), three_quarters(src.at[1, 1]))
 
     def from_next_corner():
-        wires.wait(("next corner", 0), src.at[1, 3])
-
-    def cast(s, carry):
-        amps[0][0][s] = start[s].astype(BF16)
-        return carry
-
-    late = ((2, 0), (2, 1), (3, 0), (3, 1))
-
-    pl.semaphore_wait(barrier, 4 + inner)
-
-    def nearby_is_in():
-        pl.semaphore_signal(nearby, inc=1, device_id=to_partner, device_id_type=MESH)
-
-    pl.when(mid)(nearby_is_in)
-    wires.start(("d", 1), dom.at[0, 0], dom.at[0, 1], to_mate)
-    wires.start(("d", 2), dom.at[0, 0], dom.at[0, 2], to_across)
-    for i in (2, 3, 0, 1):
+        wires.wait(("next corner", 1), src.at[1, 3, four(g)])
+
+    def from_next_corner_rest():
+        wires.wait(("next corner", 0), three_quarters(src.at[1, 3]))
+
+    def own_across(i):
         part = four(groups[i])
         wires.start(
             ("own across", i), c_ref.at[part], src.at[0, 2, part], to_across, None,
             ("own across", 0), c_ref,
         )
+
+    def cast(s, carry):
+        amps[0][0][s] = start[s].astype(BF16)
+        return carry
+
+    pl.semaphore_wait(barrier, 4 + inner)
+    wires.start(("d", 1), dom.at[0, 0], dom.at[0, 1], to_mate)
+    wires.start(("d", 2), dom.at[0, 0], dom.at[0, 2], to_across)
+    own_across(2)
+    to_next(0)
+    ready(0)
     for i in (1, 0, 2, 3):
         part = four(groups[i])
         wires.start(
             ("own mate", int(i == 1)), c_ref.at[part], src.at[0, 1, part], to_mate, None,
             ("own mate", 0), c_ref,
         )
-    pl.when(end)(lambda: pl.semaphore_wait(nearby, 1))
-    ready(0)
+    own_across(3)
+    own_across(0)
+    for i in (2, 3, 1):
+        to_next(i)
     from_mate()
     turn(1)
     ready(1)
-    to_next(0)
-    to_next(1)
+    wires.wait(("d", 1), dom.at[0, 1])
+    wires.wait(("d", 2), dom.at[0, 2])
+    wires.start(("d", 3), dom.at[0, 2], dom.at[0, 3], to_mate)
     for load in (load_owner, load_slot, load_fock):
         load.wait()
     lax.fori_loop(0, quarter, table, 0)
-    wires.wait(("d", 1), dom.at[0, 1])
-    wires.wait(("d", 2), dom.at[0, 2])
-    wires.start(("d", 3), dom.at[0, 2], dom.at[0, 3], to_mate)
-    load_start.wait()
-    lax.fori_loop(0, pc, cast, 0, unroll=2)
+    ready("slot")
+    ready("fock")
     wires.wait(("d", 3), dom.at[0, 3])
     for rel in range(4):
         for t in range(quarter):
             bdom[0, rel * quarter + t] = dom[0, rel, g * quarter + t]
+    ready("dom")
     wires.start(("d", 4), dom.at[0], dom.at[1], to_partner)
-    for kind in small:
-        ready(kind)
+    from_next(0)
+    turn(0, 1)
+    next_ready(0)
+    got_first(0)
     from_across(0)
     turn(2)
-    got_first(0)
-    got_second(0)
+    ready(2)
     expand(0, 0)
+    from_next(2)
+    own_across(1)
     from_across(1)
+    got_first(1)
     from_corner()
     turn(3)
-    to_next(2)
-    share_partner(0, 0)
-    share_partner(0, 1)
-    to_next(3)
-    for kind in late:
-        ready(kind)
-    got_first(1)
-    got_second(1)
+    ready(3)
+    load_start.wait()
+    lax.fori_loop(0, pc, cast, 0, unroll=2)
+    from_next(3)
     from_across(2)
-    from_next(0)
+    to_wide(2)
+    share_start(0)
+    got_further(0)
     from_mate_rest()
     expand(0, 1)
+    from_next(1)
+    from_next_across(0)
+    turn(2, 1)
+    next_ready(2)
+    from_next_mate()
+    turn(1, 1)
+    next_ready(1)
+    got_first(2)
     from_across(3)
-    from_next(1)
+    to_wide(3)
+    share_start(1)
     for kind in small:
         got_first(kind)
+    wires.wait(("d", 4), dom.at[1])
+    for rel in range(4):
+        for t in range(quarter):
+            bdom[1, rel * quarter + t] = dom[1, rel, g * quarter + t]
+    next_ready("dom")
+    next_ready("slot")
+    next_ready("fock")
+    got_first(3)
+    from_wide(2)
+    from_next_across(1)
     from_corner_rest()
-    from_next_across(2)
-    for kind in late:
-        got_first(kind)
     expand(0, 2)
-    from_next(2)
+    from_next_corner()
+    turn(3, 1)
+    next_ready((3, 0))
+    next_ready((3, 1))
+    pass_start(0)
+    got_further(2)
     expand(0, 3)
-    for h in (0, 1):
-        pass_partner(0, h)
-    from_next_across(3)
-    wires.wait(("d", 4), dom.at[1])
-    from_next(3)
     for kind in small:
-        got_second(kind)
-    from_next_mate()
-    expand(1, 0)
-    from_next_across(0)
+        got_further(kind)
     make_turned(0)
     make_x(0, 0)
-    for kind in ((2, 0), (2, 1)):
-        got_second(kind)
-    pass_across(0, 0)
-    pass_across(0, 1)
+    got_further(1)
+    from_wide(3)
+    expand(1, 0)
+    from_next_mate_rest()
+    expand(1, 1)
+    from_next_corner_rest()
+    expand(1, 2)
+    pass_start(1)
     got_beside()
+    got_further((3, 0))
+    expand(1, 3)
+    got_further((3, 1))
+    make_x(0, 1)
     make_turned(1)
     make_x(1, 0)
-    for kind in ((3, 0),):
-        got_second(kind)
-    from_next_across(1)
-    for kind in ((3, 1),):
-        got_second(kind)
-    expand(1, 1)
+    make_x(1, 1)
     have_partner(0)
-    from_next_corner()
-    expand(1, 2)
-    expand(1, 3)
-    make_x(1, 1)
     couple(1, 0, 0)
     couple(1, 1, 0)
     post(0, 0)
@@ -993,7 +1064,8 @@
     make_x(2, 1)
     couple(2, 0, 0)
     couple(2, 1, 0)
-    make_x(0, 1)
+    couple(0, 0, 0)
+    couple(0, 1, 0)
     got_beside2()
     make_turned(3)
     make_x(3, 0)
@@ -1001,8 +1073,6 @@
     couple(3, 0, 0)
     couple(3, 1, 0)
     post(0, 1)
-    couple(0, 0, 0)
-    couple(0, 1, 0)
     for load in (load_k, load_e, load_shift):
         load.wait()
     sum_first(0)
@@ -1010,30 +1080,19 @@
 
     for t in range(quarter):
         amps[1][0][g * quarter + t] = updated(0, t)
-        if t % half_quarter == half_quarter - 1:
-            h = t // half_quarter
-            part = two(g, h)
-            ref = amps[1][0].at[part]
-            share_partner(1, h)
-            wires.start(
-                ("own", 1, h), ref, ref, to_across, None, ("own", 1), amps[1][0].at[four(g)]
-            )
-            wires.start(
-                ("own", 2), ref, ref, to_mate, None, ("own", 2), both_quarters(amps[1][0])
-            )
-    for h in (0, 1):
-        pass_partner(1, h)
-        part = two(across, h)
-        wires.wait(("own", 1, h), amps[1][0].at[part])
-        ref = amps[1][0].at[part]
-        wires.start(("own", 2), ref, ref, to_mate, None, ("own", 2), both_quarters(amps[1][0]))
+        share(t)
+    for t in range(quarter):
+        pass_partner(t)
+        pass_own(t)
     wires.wait(("own", 2), both_quarters(amps[1][0]))
     couple(3, 0, 1)
     couple(1, 0, 1)
-    pass_across(1, 0)
+    for t in range(half_quarter):
+        pass_across(t)
     couple(2, 0, 1)
-    pass_across(1, 1)
     couple(0, 0, 1)
+    for t in range(half_quarter, quarter):
+        pass_across(t)
     have_partner(1)
     couple(3, 1, 1)
     post(1, 1)
@@ -1048,22 +1107,19 @@
         value = coupled(1, t).astype(BF16)
         mine[t] = value
         out_ref[g * quarter + t] = value
-        if t % half_quarter == half_quarter - 1:
-            h = t // half_quarter
-            part = mine.at[pl.ds(h * half_quarter, half_quarter)]
-            dst = out_ref.at[two(g, h)]
-            wires.start(("out", 1, h), part, dst, to_across, None, ("out", 1), mine)
-            wires.start(("out", 2), part, dst, to_mate, None, ("out", 2), both_quarters(out_ref))
-    for h in (0, 1):
-        ref = out_ref.at[two(across, h)]
-        wires.wait(("out", 1, h), ref)
+        part, dst = mine.at[t], out_ref.at[g * quarter + t]
+        wires.start(("out", 1, t), part, dst, to_across, None, ("out", 1), mine)
+        wires.start(("out", 2), part, dst, to_mate, None, ("out", 2), both_quarters(out_ref))
+    for t in range(quarter):
+        ref = out_ref.at[across * quarter + t]
+        wires.wait(("out", 1, t), ref)
         wires.start(("out", 2), ref, ref, to_mate, None, ("out", 2), both_quarters(out_ref))
     wires.wait(("out", 2), both_quarters(out_ref))
     wires.drain()
     assert len(wires.sends) <= SENDS and len(wires.recvs) <= RECVS, (len(wires.sends), len(wires.recvs))
 
 
-SENDS, RECVS = 45, 96
+SENDS, RECVS = 50, 120
 
 
 def quadrants_fit(n, groups, pc):
@@ -1110,7 +1166,7 @@
             pltpu.VMEM((2, 2, quarter, *big), BF16),
             pltpu.VMEM((2, 2, quarter, *big), BF16),
             pltpu.VMEM((quarter, *big), BF16),
-            dma((SENDS,)), dma((RECVS,)), dma((9,)), pltpu.SemaphoreType.REGULAR,
+            dma((SENDS,)), dma((RECVS,)), dma((9,)),
         ],
         compiler_params=pltpu.CompilerParams(
             collective_id=0, has_side_effects=True, vmem_limit_bytes=60 * 2**20

time: 78.2 us -> 71.6 us (0.916)
  Pallas kernels: 75.6 us -> 69 us
    pallas_call x1, Pallas kernels: 75.6 us -> 69 us  [quadrants_call(): pl.pallas_call(functools.partial(quadrants_kernel, n), out_shape=jax.Shap...]
where the time goes in v3:
time: 71.6 us; the launch traced here: 71.4 us
  Pallas kernels  69 us (96%)
  other arithmetic  2.38 us (3%)
    pallas_call x1, Pallas kernels, quadrants_call(): pl.pallas_call(functools.partial(quadrants_kernel, n), out_shape=jax.Shap...  69 us
    div x1, other arithmetic, quadrants_call(): return -(integrals + total.astype(F32)) / denominator  2.38 us

profile of v3, /device:TPU:0, one launch (start us, length us, event | category | flops | bytes accessed | tf_op | source)
XLA Modules:
  0.0 71.4 jit_solution(14445238810583229799)
XLA Ops:
  0.0 0.0 copy-start
  0.0 0.0 copy-start.1
  0.0 0.0 copy-start.2
  0.0 69.0 %quadrants.1 = bf16[16,128,128]{2,1,0:T(8,128)(2,1)} custom-call(s32[8,16]{1,0:T(8,128)} %bitcast.3, s32[8,16]{1,0:T(8,128)} %bitcast.4, f32[8,16]{1,0:T(8,128)} %bitcast.5, f32[16]{0:T(128)} %refs_3_.1, bf16[16,128,128]{2,1,0:T(8,128)(2,1)} %refs_4_.1, s32[16,128]{1,0:T(8,128)} %refs_5_.1, f32[16,128,128]{2,1,0:T(8,128)} %refs_6_.1, ...), custom_call_target="tpu_custom_call" | custom-call | tf_op jit(solution)/shard_map/quadrants/pallas_call | solution.py:1141
  69.0 0.0 copy-done
  69.1 0.0 copy-done.1
  69.1 0.0 copy-done.2
  69.1 2.4 %add_divide_fusion = f32[16,128,128]{2,1,0:T(8,128)} fusion(f32[16,128,128]{2,1,0:T(8,128)S(1)} %copy-done, bf16[16,128,128]{2,1,0:T(8,128)(2,1)} %quadrants.1, f32[16]{0:T(128)S(1)} %copy-done.2, f32[16,128]{1,0:T(8,128)S(1)} %copy-done.1), kind=kLoop, calls=%fused_computation | loop fusion | flops 1572864 | bytes 2629696 | tf_op jit(solution)/shard_map/div | solution.py:1177
Async XLA Ops:
  0.0 69.0 %copy-start = (f32[16,128,128]{2,1,0:T(8,128)S(1)}, f32[16,128,128]{2,1,0:T(8,128)}, u32[]{:S(2)}) copy-start(f32[16,128,128]{2,1,0:T(8,128)} %refs_7_.1) | copy-start | bytes 3145732
  0.0 69.0 %copy-start.1 = (f32[16,128]{1,0:T(8,128)S(1)}, f32[16,128]{1,0:T(8,128)}, u32[]{:S(2)}) copy-start(f32[16,128]{1,0:T(8,128)} %refs_8_.1) | copy-start | bytes 24580
  0.0 69.1 %copy-start.2 = (f32[16]{0:T(128)S(1)}, f32[16]{0:T(128)}, u32[]{:S(2)}) copy-start(f32[16]{0:T(128)} %refs_3_.1) | copy-start | bytes 196

commit v4 on v3

--- a/solution.py
+++ b/solution.py
@@ -487,35 +487,24 @@
 class Wires:
     def __init__(self, send, recv, here):
         self.send, self.recv, self.here = send, recv, here
-        self.sends, self.recvs, self.wholes = {}, {}, {}
-
-    def link(self, key, src, dst, peer, out=None):
-        out = key if out is None else out
+        self.sends, self.recvs = {}, {}
+
+    def link(self, key, src, dst, peer, out):
         at_send = self.sends.setdefault(out, len(self.sends))
         at_recv = self.recvs.setdefault(key, len(self.recvs))
         return remote(src, dst, self.send.at[at_send], self.recv.at[at_recv], peer)
 
-    def start_in(self, when, key, src, dst, peer, out=None, whole=None):
+    def start_in(self, when, key, src, dst, peer, out):
         self.link(key, src, dst, peer, out).start()
-        out = key if out is None else out
-        role = 0 if when is None else 1 + (when is self.mid)
-        self.wholes[out, role] = (src if whole is None else whole, when)
-
-    def start(self, key, src, dst, peer, when=None, out=None, whole=None):
+
+    def start(self, key, src, dst, peer, out, when=None):
         def run():
-            self.start_in(when, key, src, dst, peer, out, whole)
+            self.start_in(when, key, src, dst, peer, out)
 
         if when is None:
             run()
         else:
             pl.when(when)(run)
-
-    def start_all(self, when, jobs):
-        def run():
-            for job in jobs:
-                self.start_in(when, *job)
-
-        pl.when(when)(run)
 
     def wait(self, key, dst, when=None):
         at_recv = self.recvs.setdefault(key, len(self.recvs))
@@ -525,14 +514,13 @@
         else:
             pl.when(when)(copy.wait_recv)
 
-    def drain(self):
-        for (out, _), (whole, when) in self.wholes.items():
-            at_send = self.sends[out]
-            copy = remote(whole, whole, self.send.at[at_send], self.recv.at[0], self.here)
-            if when is None:
-                copy.wait_send()
-            else:
-                pl.when(when)(copy.wait_send)
+    def drain(self, out, whole, when=None):
+        at_send = self.sends[out]
+        copy = remote(whole, whole, self.send.at[at_send], self.recv.at[0], self.here)
+        if when is None:
+            copy.wait_send()
+        else:
+            pl.when(when)(copy.wait_send)
 
 
 def note(*what):
@@ -598,14 +586,14 @@
         return ref.at[pl.ds(0, 3 * quarter)]
 
     def source(b, rel):
-        return c_ref if (b, rel) == (0, 0) else src.at[b, rel]
+        return c_ref if (b, rel) == (0, 0) else src.at[4 * b + rel]
 
     def turn(rel, b=0):
         for t in range(quarter):
             blocks[b, rel, t] = source(b, rel)[g * quarter + t].T
 
     for s in range(pc):
-        dom[0, 0, s] = dom_ref[pl.ds(s, 1), :]
+        dom[0, s] = dom_ref[pl.ds(s, 1), :]
     turn(0)
 
     def table(t, carry):
@@ -637,52 +625,44 @@
             )
         kinds[rel] = functools.partial(lambda rel, b: blocks.at[b, rel], rel)
 
-    def grouped(kind, ref):
-        return (ref, kind) if kind in small else (blocks.at[0], 0)
+    def tag(kind):
+        return kind if kind in small else "targets"
+
+    def landing(kind):
+        return kind if kind in small or kind in ((3, 0), (3, 1)) else 0
 
     def ready(kind):
         ref = kinds[kind](0)
-        whole, tag = grouped(kind, ref)
-        together = ("beside", tag)
+        onward, across_cut = kinds[kind](4), kinds[kind](2)
         if kind in ("slot", "fock"):
-            wires.start(("second", kind), ref, kinds[kind](1), to_partner)
-        wires.start_all(end, [(together, ref, kinds[kind](4), to_beside, together, whole)])
-        wires.start_all(
-            mid, [(("cross", kind), ref, kinds[kind](2), to_cross, ("cross", tag), whole)]
-        )
+            wires.start(("second", kind), ref, kinds[kind](1), to_partner, kind)
+        wires.start(("beside", 0 if tag(kind) == "targets" else kind), ref, onward, to_beside, tag(kind), end)
+        wires.start(("cross", kind), ref, across_cut, to_cross, tag(kind), mid)
 
     def next_ready(kind):
         ref = kinds[kind](1)
-        whole, tag = grouped(kind, ref)
-        together = ("beside2", tag)
+        onward, across_cut = kinds[kind](5), kinds[kind](3)
         if kind in ("slot", "fock"):
             wires.wait(("second", kind), ref)
-        wires.start_all(end, [(together, ref, kinds[kind](5), to_beside, together, whole)])
-        wires.start_all(
-            mid, [(("further", kind), ref, kinds[kind](3), to_cross, ("further", tag), whole)]
-        )
-
-    first, second = 2 * inner, 1 + 2 * inner
+        wires.start(("beside2", landing(kind)), ref, onward, to_beside, tag(kind), end)
+        wires.start(("further", kind), ref, across_cut, to_cross, tag(kind), mid)
 
     def got_first(kind):
         landed, passed = kinds[kind](2), kinds[kind](4)
-        whole, tag = grouped(kind, landed)
-        together = ("beside", tag)
 
         def relay():
             wires.wait(("cross", kind), landed)
-            wires.start_in(mid, together, landed, passed, to_beside, together, whole)
+            key = ("beside", 0 if tag(kind) == "targets" else kind)
+            wires.start_in(mid, key, landed, passed, to_beside, tag(kind))
 
         pl.when(mid)(relay)
 
     def got_further(kind):
         landed, passed = kinds[kind](3), kinds[kind](5)
-        whole, tag = grouped(kind, landed)
-        together = ("beside2", tag)
 
         def relay():
             wires.wait(("further", kind), landed)
-            wires.start_in(mid, together, landed, passed, to_beside, together, whole)
+            wires.start_in(mid, ("beside2", landing(kind)), landed, passed, to_beside, tag(kind))
 
         pl.when(mid)(relay)
 
@@ -694,8 +674,9 @@
     def got_beside2():
         for kind in small:
             wires.wait(("beside2", kind), kinds[kind](5))
-        wires.wait(("beside2", 0), blocks.at[5])
-
+        wires.wait(("beside2", 0), blocks.at[5, pl.ds(0, 3)])
+
+    first, second = 2 * inner, 1 + 2 * inner
     places_of = (first, 4, second, 5)
 
     lines = lax.broadcasted_iota(jnp.int16, (NB, rows), 0)
@@ -710,7 +691,7 @@
         block = source(b, rel)
 
         def one(s, carry):
-            hit = one_hot(lines, dom[b, rel, s] - base)
+            hit = one_hot(lines, dom[4 * b + rel, s] - base)
             wide[b, s, pl.ds(rel * NB, NB)] = jnp.dot(
                 hit, block[s], preferred_element_type=F32
             ).astype(BF16)
@@ -725,8 +706,11 @@
             for t in range(quarter):
                 one(groups[i] * quarter + t, 0)
 
-    def make_turned(b, hs=(0, 1)):
-        note("make_turned", b)
+    every = tuple(range(quarter))
+    early, later = every[:half_quarter], every[half_quarter:]
+
+    def make_turned(b, hs=(0, 1), ts=every):
+        note("make_turned", b, 0, len(hs) * len(ts) / 8)
         place = places_of[b]
 
         def one(t, carry):
@@ -746,12 +730,16 @@
                 ).astype(BF16)
             return carry
 
-        lax.fori_loop(0, quarter, one, 0, unroll=2)
+        if ts == every:
+            lax.fori_loop(0, quarter, one, 0, unroll=2)
+        else:
+            for t in ts:
+                one(t, 0)
 
     owners = (p, partner)
 
-    def make_x(b, s):
-        note("make_x", b, s)
+    def make_x(b, s, ts=every):
+        note("make_x", b, s, len(ts) / 4)
         place = places_of[b]
 
         def one(t, carry):
@@ -761,13 +749,14 @@
             ).astype(BF16)
             return carry
 
-        lax.fori_loop(0, quarter, one, 0, unroll=4)
-
-    def couple(b, s, it):
-        note("couple", b, s)
+        for t in ts:
+            one(t, 0)
+
+    def couple(b, s, it, ts=every):
+        note("couple", b, s, len(ts) / 4)
         place = places_of[b]
         found = []
-        for t in range(quarter):
+        for t in ts:
             at_source = bslot[place, t, owners[s]]
             xs = x[b, t, s]
             half = jnp.dot(xs, amps[it][s][at_source], preferred_element_type=F32).astype(BF16)
@@ -782,47 +771,44 @@
             else:
                 yout[it, b // 2, t] = (acc[b, t] + y).astype(BF16)
 
-    def post(it, m):
-        for t in range(quarter):
-            wires.start(
-                ("y", it, m, t), yout.at[it, m, t], yx.at[it, m, t], to_beside, None,
-                ("y", it, m), yout.at[it, m],
-            )
+    def post(it, m, ts=every):
+        for t in ts:
+            wires.start(("y", it, m, t), yout.at[it, m, t], yx.at[it, m, t], to_beside, "y")
 
     def share(t):
         at_pair = g * quarter + t
-        ref, part = amps[1][0].at[at_pair], amps[1][0].at[four(g)]
-        wires.start(("a", 1, 0, t), ref, amps[1][1].at[at_pair], to_partner, None, ("a", 1, 0), part)
-        wires.start(("own", 1, t), ref, ref, to_across, None, ("own", 1), part)
-        wires.start(("own", 2), ref, ref, to_mate, None, ("own", 2), both_quarters(amps[1][0]))
+        ref = amps[1][0].at[at_pair]
+        wires.start(("own", 1, t), ref, ref, to_across, "amps")
+        wires.start(("own", 2), ref, ref, to_mate, "amps")
+
+    def share_partner(t, when):
+        at_pair = g * quarter + t
+        wires.start(("a", 1, 0, t), amps[1][0].at[at_pair], amps[1][1].at[at_pair], to_partner, "amps", when)
 
     def pass_partner(t):
-        ref, part = amps[1][1].at[g * quarter + t], amps[1][1].at[four(g)]
+        ref = amps[1][1].at[g * quarter + t]
         wires.wait(("a", 1, 0, t), ref)
-        wires.start(("a", 1, 1, t), ref, ref, to_across, None, ("a", 1, 1), part)
-        wires.start(("a", 1, 2), ref, ref, to_mate, None, ("a", 1, 2), both_quarters(amps[1][1]))
+        wires.start(("a", 1, 1, t), ref, ref, to_across, "amps")
+        wires.start(("a", 1, 2), ref, ref, to_mate, "amps")
 
     def pass_own(t):
         ref = amps[1][0].at[across * quarter + t]
         wires.wait(("own", 1, t), ref)
-        wires.start(("own", 2), ref, ref, to_mate, None, ("own", 2), both_quarters(amps[1][0]))
+        wires.start(("own", 2), ref, ref, to_mate, "amps")
 
     def pass_across(t):
         ref = amps[1][1].at[across * quarter + t]
         wires.wait(("a", 1, 1, t), ref)
-        wires.start(("a", 1, 2), ref, ref, to_mate, None, ("a", 1, 2), both_quarters(amps[1][1]))
+        wires.start(("a", 1, 2), ref, ref, to_mate, "amps")
 
     def share_start(j):
         part = four((g, across)[j])
-        wires.start(
-            ("start", j), amps[0][0].at[part], amps[0][1].at[part], to_partner, None,
-            ("start", 0), both_quarters(amps[0][0]),
-        )
+        wires.start(("start", j), amps[0][0].at[part], amps[0][1].at[part], to_partner, "amps")
 
     def pass_start(j):
         ref = amps[0][1].at[four((g, across)[j])]
         wires.wait(("start", j), ref)
-        wires.start(("a", 0, 2), ref, ref, to_mate, None, ("a", 0, 2), both_quarters(amps[0][1]))
+        wires.start(("a", 0, 2), ref, ref, to_mate, "amps")
 
     def have_partner(it):
         wires.wait(("a", it, 2), both_quarters(amps[it][1]))
@@ -832,20 +818,16 @@
             wires.wait(("y", it, 1, t), yx.at[it, 1, t])
             ysum[it, 1, t] = (acc[2, t] + yx[it, 1, t].astype(F32)).astype(BF16)
             job = (("yfar", it, t), ysum.at[it, 1, t], yin.at[it, 0, t])
-            group = (("yfar", it), ysum.at[it, 1])
-            wires.start_all(end, [(*job, to_partner, *group)])
-            wires.start_all(mid, [(*job, to_far, *group)])
-
-    def sum_first(it):
-        for t in range(quarter):
+            wires.start(*job, to_partner, "yfar", end)
+            wires.start(*job, to_far, "yfar", mid)
+
+    def sum_first(it, ts=every):
+        for t in ts:
             wires.wait(("y", it, 0, t), yx.at[it, 0, t])
             total = acc[0, t] + yx[it, 0, t].astype(F32)
             acc[0, t] = total
             ysum[it, 0, t] = total.astype(BF16)
-            wires.start_all(mid, [(
-                ("ynear", it, t), ysum.at[it, 0, t], yin.at[it, 1, t], to_cross,
-                ("ynear", it), ysum.at[it, 0],
-            )])
+            wires.start(("ynear", it, t), ysum.at[it, 0, t], yin.at[it, 1, t], to_cross, "ynear", mid)
 
     def coupled(it, t):
         wires.wait(("ynear", it, t), yin.at[it, 1, t], mid)
@@ -862,84 +844,79 @@
     swap_mate, swap_across = (1, 0, 3, 2), (2, 3, 0, 1)
 
     def from_mate():
-        wires.wait(("own mate", 1), src.at[0, 1, four(g)])
+        wires.wait(("own mate", 1), src.at[1, four(g)])
 
     def from_mate_rest():
-        wires.wait(("own mate", 0), three_quarters(src.at[0, 1]))
+        wires.wait(("own mate", 0), three_quarters(src.at[1]))
 
     def from_across(i):
         part = four(groups[i])
-        wires.wait(("own across", swap_across[i]), src.at[0, 2, part])
+        wires.wait(("own across", swap_across[i]), src.at[2, part])
         wires.start(
-            ("own corner", int(i == 1)), src.at[0, 2, part], src.at[0, 3, part], to_mate, None,
-            ("own corner", 0), src.at[0, 2],
+            ("own corner", int(i == 1)), src.at[2, part], src.at[3, part], to_mate,
+            "rows",
         )
 
     def from_corner():
-        wires.wait(("own corner", 1), src.at[0, 3, four(g)])
+        wires.wait(("own corner", 1), src.at[3, four(g)])
 
     def from_corner_rest():
-        wires.wait(("own corner", 0), three_quarters(src.at[0, 3]))
+        wires.wait(("own corner", 0), three_quarters(src.at[3]))
 
     def to_next(i):
         part = four(groups[i])
         wires.start(
-            ("next", i), c_ref.at[part], src.at[1, 0, part], to_partner, None, ("next", 0), c_ref
+            ("next", i), c_ref.at[part], src.at[4, part], to_partner, "rows"
         )
 
     def from_next(i):
         part = four(groups[i])
-        ref = src.at[1, 0, part]
+        ref = src.at[4, part]
         wires.wait(("next", i), ref)
-        if i in (2, 3):
+        if i > 0:
             wires.start(
-                ("next across", i), ref, src.at[1, 2, part], to_across, None,
-                ("next across", 0), both_quarters(src.at[1, 0]),
+                ("next across", i), ref, src.at[6, part], to_across, "rows",
             )
         wires.start(
-            ("next mate", int(i == 1)), ref, src.at[1, 1, part], to_mate, None,
-            ("next mate", 0), src.at[1, 0],
+            ("next mate", int(i == 1)), ref, src.at[5, part], to_mate, "rows",
         )
 
     def to_wide(i):
         part = four(groups[i])
         wires.start(
-            ("next wide", i), src.at[0, 2, part], src.at[1, 2, part], to_partner, None,
-            ("next wide", 0), both_quarters(src.at[0, 2]),
+            ("next wide", i), src.at[2, part], src.at[6, part], to_partner, "rows",
         )
 
     def corner(i):
         part = four(groups[i])
         wires.start(
-            ("next corner", int(i == 1)), src.at[1, 2, part], src.at[1, 3, part], to_mate, None,
-            ("next corner", 0), src.at[1, 2],
+            ("next corner", int(i == 1)), src.at[6, part], src.at[7, part], to_mate, "rows",
         )
 
     def from_next_across(i):
-        wires.wait(("next across", swap_across[i]), src.at[1, 2, four(groups[i])])
+        wires.wait(("next across", swap_across[i]), src.at[6, four(groups[i])])
         corner(i)
 
     def from_wide(i):
-        wires.wait(("next wide", i), src.at[1, 2, four(groups[i])])
+        wires.wait(("next wide", i), src.at[6, four(groups[i])])
         corner(i)
 
     def from_next_mate():
-        wires.wait(("next mate", 1), src.at[1, 1, four(g)])
+        wires.wait(("next mate", 1), src.at[5, four(g)])
 
     def from_next_mate_rest():
-        wires.wait(("next mate", 0), three_quarters(src.at[1, 1]))
+        wires.wait(("next mate", 0), three_quarters(src.at[5]))
 
     def from_next_corner():
-        wires.wait(("next corner", 1), src.at[1, 3, four(g)])
+        wires.wait(("next corner", 1), src.at[7, four(g)])
 
     def from_next_corner_rest():
-        wires.wait(("next corner", 0), three_quarters(src.at[1, 3]))
+        wires.wait(("next corner", 0), three_quarters(src.at[7]))
 
     def own_across(i):
         part = four(groups[i])
         wires.start(
-            ("own across", i), c_ref.at[part], src.at[0, 2, part], to_across, None,
-            ("own across", 0), c_ref,
+            ("own across", i), c_ref.at[part], src.at[2, part], to_across, "rows",
         )
 
     def cast(s, carry):
@@ -947,139 +924,162 @@
         return carry
 
     pl.semaphore_wait(barrier, 4 + inner)
-    wires.start(("d", 1), dom.at[0, 0], dom.at[0, 1], to_mate)
-    wires.start(("d", 2), dom.at[0, 0], dom.at[0, 2], to_across)
+    wires.start(("d", 1), dom.at[0], dom.at[1], to_mate, "doms")
+    wires.start(("d", 2), dom.at[0], dom.at[2], to_across, "doms")
     own_across(2)
     to_next(0)
-    ready(0)
+    ready((0, 0))
+    ready((0, 1))
     for i in (1, 0, 2, 3):
         part = four(groups[i])
         wires.start(
-            ("own mate", int(i == 1)), c_ref.at[part], src.at[0, 1, part], to_mate, None,
-            ("own mate", 0), c_ref,
+            ("own mate", int(i == 1)), c_ref.at[part], src.at[1, part], to_mate, "rows",
         )
     own_across(3)
     own_across(0)
-    for i in (2, 3, 1):
-        to_next(i)
+    to_next(2)
     from_mate()
     turn(1)
     ready(1)
-    wires.wait(("d", 1), dom.at[0, 1])
-    wires.wait(("d", 2), dom.at[0, 2])
-    wires.start(("d", 3), dom.at[0, 2], dom.at[0, 3], to_mate)
+    wires.wait(("d", 1), dom.at[1])
+    wires.wait(("d", 2), dom.at[2])
+    wires.start(("d", 3), dom.at[2], dom.at[3], to_mate, "doms")
     for load in (load_owner, load_slot, load_fock):
         load.wait()
     lax.fori_loop(0, quarter, table, 0)
     ready("slot")
     ready("fock")
-    wires.wait(("d", 3), dom.at[0, 3])
+    wires.wait(("d", 3), dom.at[3])
+    wires.start(("d", 4), dom.at[pl.ds(0, 4)], dom.at[pl.ds(4, 4)], to_partner, "doms")
+    to_next(3)
+    to_next(1)
     for rel in range(4):
         for t in range(quarter):
-            bdom[0, rel * quarter + t] = dom[0, rel, g * quarter + t]
+            bdom[0, rel * quarter + t] = dom[rel, g * quarter + t]
     ready("dom")
-    wires.start(("d", 4), dom.at[0], dom.at[1], to_partner)
+    got_first((0, 0))
+    expand(0, 0)
     from_next(0)
     turn(0, 1)
     next_ready(0)
-    got_first(0)
+    got_first((0, 1))
     from_across(0)
     turn(2)
-    ready(2)
-    expand(0, 0)
+    ready((2, 0))
+    ready((2, 1))
+    from_mate_rest()
+    expand(0, 1)
+    expand(0, 2, (0,))
     from_next(2)
     own_across(1)
+    got_first(1)
     from_across(1)
-    got_first(1)
     from_corner()
     turn(3)
-    ready(3)
+    ready((3, 0))
+    ready((3, 1))
     load_start.wait()
     lax.fori_loop(0, pc, cast, 0, unroll=2)
-    from_next(3)
+    wires.wait(("d", 4), dom.at[pl.ds(4, 4)])
+    expand(0, 2, (1,))
+    expand(1, 0, (0, 2))
     from_across(2)
     to_wide(2)
     share_start(0)
+    share_start(1)
     got_further(0)
-    from_mate_rest()
-    expand(0, 1)
+    from_next(3)
+    expand(0, 2, (2,))
+    expand(1, 0, (3,))
+    got_first((2, 0))
+    for rel in range(4):
+        for t in range(quarter):
+            bdom[1, rel * quarter + t] = dom[4 + rel, g * quarter + t]
+    next_ready("dom")
+    next_ready("slot")
+    next_ready("fock")
     from_next(1)
     from_next_across(0)
     turn(2, 1)
-    next_ready(2)
+    next_ready((2, 0))
+    next_ready((2, 1))
+    got_first((2, 1))
+    expand(1, 0, (1,))
     from_next_mate()
     turn(1, 1)
-    next_ready(1)
-    got_first(2)
+    next_ready((1, 0))
+    next_ready((1, 1))
+    got_first((3, 0))
+    from_next_mate_rest()
+    expand(1, 1)
+    got_first((3, 1))
     from_across(3)
-    to_wide(3)
-    share_start(1)
     for kind in small:
         got_first(kind)
-    wires.wait(("d", 4), dom.at[1])
-    for rel in range(4):
-        for t in range(quarter):
-            bdom[1, rel * quarter + t] = dom[1, rel, g * quarter + t]
-    next_ready("dom")
-    next_ready("slot")
-    next_ready("fock")
-    got_first(3)
+    expand(1, 2, (0,))
     from_wide(2)
+    got_further((2, 0))
+    expand(0, 2, (3,))
+    expand(1, 2, (2,))
+    from_corner_rest()
+    got_further((2, 1))
+    expand(0, 3)
     from_next_across(1)
-    from_corner_rest()
-    expand(0, 2)
     from_next_corner()
     turn(3, 1)
     next_ready((3, 0))
     next_ready((3, 1))
+    got_further((1, 0))
     pass_start(0)
-    got_further(2)
-    expand(0, 3)
+    expand(1, 2, (1,))
+    make_turned(0)
+    got_further((1, 1))
+    from_next_across(3)
+    make_x(0, 0)
+    expand(1, 2, (3,))
+    pass_start(1)
     for kind in small:
         got_further(kind)
-    make_turned(0)
-    make_x(0, 0)
-    got_further(1)
-    from_wide(3)
-    expand(1, 0)
-    from_next_mate_rest()
-    expand(1, 1)
     from_next_corner_rest()
-    expand(1, 2)
-    pass_start(1)
+    expand(1, 3)
+    got_further((3, 0))
     got_beside()
-    got_further((3, 0))
-    expand(1, 3)
-    got_further((3, 1))
-    make_x(0, 1)
     make_turned(1)
     make_x(1, 0)
     make_x(1, 1)
     have_partner(0)
+    got_further((3, 1))
     couple(1, 0, 0)
     couple(1, 1, 0)
-    post(0, 0)
+    post(0, 0, early)
     make_turned(2)
     make_x(2, 0)
     make_x(2, 1)
     couple(2, 0, 0)
     couple(2, 1, 0)
+    got_beside2()
+    make_turned(3, (0,))
+    for h, ts in ((0, early), (1, later)):
+        wires.wait(("beside2", (3, h)), kinds[3, h](5))
+        make_turned(3, (1,), ts)
+        make_x(3, 0, ts)
+        make_x(3, 1, ts)
+        couple(3, 0, 0, ts)
+        couple(3, 1, 0, ts)
+        post(0, 1, ts)
+    post(0, 0, later)
+    make_x(0, 1)
     couple(0, 0, 0)
     couple(0, 1, 0)
-    got_beside2()
-    make_turned(3)
-    make_x(3, 0)
-    make_x(3, 1)
-    couple(3, 0, 0)
-    couple(3, 1, 0)
-    post(0, 1)
     for load in (load_k, load_e, load_shift):
         load.wait()
-    sum_first(0)
+    sum_first(0, early)
     sum_second(0)
+    sum_first(0, later)
 
     for t in range(quarter):
         amps[1][0][g * quarter + t] = updated(0, t)
+        share_partner(t, None)
         share(t)
     for t in range(quarter):
         pass_partner(t)
@@ -1108,22 +1108,33 @@
         mine[t] = value
         out_ref[g * quarter + t] = value
         part, dst = mine.at[t], out_ref.at[g * quarter + t]
-        wires.start(("out", 1, t), part, dst, to_across, None, ("out", 1), mine)
-        wires.start(("out", 2), part, dst, to_mate, None, ("out", 2), both_quarters(out_ref))
+        wires.start(("out", 1, t), part, dst, to_across, "amps")
+        wires.start(("out", 2), part, dst, to_mate, "out")
     for t in range(quarter):
         ref = out_ref.at[across * quarter + t]
         wires.wait(("out", 1, t), ref)
-        wires.start(("out", 2), ref, ref, to_mate, None, ("out", 2), both_quarters(out_ref))
+        wires.start(("out", 2), ref, ref, to_mate, "out")
     wires.wait(("out", 2), both_quarters(out_ref))
-    wires.drain()
+    wires.drain("rows", src.at[pl.ds(0, 7)])
+    wires.drain("doms", dom.at[pl.ds(0, 7)])
+    for role, passes in ((end, 2), (mid, 4)):
+        wires.drain("targets", blocks.at[pl.ds(0, passes)], role)
+        wires.drain("dom", bdom.at[pl.ds(0, passes)], role)
+        wires.drain("slot", bslot.at[pl.ds(0, passes + 1)], role)
+        wires.drain("fock", bfock.at[pl.ds(0, passes + 1)], role)
+    wires.drain("y", yout)
+    wires.drain("yfar", ysum.at[0])
+    wires.drain("ynear", ysum.at[0], mid)
+    wires.drain("amps", src.at[pl.ds(0, 3)])
+    wires.drain("out", both_quarters(out_ref))
     assert len(wires.sends) <= SENDS and len(wires.recvs) <= RECVS, (len(wires.sends), len(wires.recvs))
 
 
-SENDS, RECVS = 50, 120
-
-
-def quadrants_fit(n, groups, pc):
-    return n == 2 * groups and groups == 4 and pc % (2 * groups) == 0
+SENDS, RECVS = 11, 110
+
+
+def quadrants_fit(n, groups, pc, rows, width):
+    return n == 2 * groups and groups == 4 and pc % (2 * groups) == 0 and rows == width
 
 
 def quadrants_kernel(n, *refs):
@@ -1148,8 +1159,8 @@
             pltpu.SMEM((ways, pc), F32), pltpu.SMEM((pc,), F32),
             pltpu.VMEM((pc, rows, width), BF16), pltpu.VMEM((pc, rows), jnp.int32),
             pltpu.VMEM((pc, width), F32),
-            pltpu.VMEM((2, 4, pc, rows, width), BF16),
-            pltpu.VMEM((2, 4, pc, 1, rows), jnp.int32),
+            pltpu.VMEM((8, pc, rows, width), BF16),
+            pltpu.VMEM((8, pc, 1, rows), jnp.int32),
             pltpu.VMEM((6, 4, quarter, width, rows), BF16),
             pltpu.VMEM((6, 4 * quarter, 1, rows), jnp.int32),
             pltpu.SMEM((6, quarter, n), jnp.int32),
@@ -1197,7 +1208,7 @@
             collective_id=collective, has_side_effects=True, vmem_limit_bytes=60 * 2**20
         )
 
-    if quadrants_fit(n, lax.axis_size("grp"), pc):
+    if quadrants_fit(n, lax.axis_size("grp"), pc, rows, width):
         return quadrants_call(
             n, coupling_owner, coupling_slot, coupling_fock, pair_shift, coefficients, domain,
             amplitudes_start, exchange_integrals, pno_energy,

time: 71.6 us -> 69 us (0.964)
  Pallas kernels: 69 us -> 66.4 us
    pallas_call x1, Pallas kernels: 69 us -> 66.4 us  [quadrants_call(): pl.pallas_call(functools.partial(quadrants_kernel, n), out_shape=jax.Shap...]
where the time goes in v4:
time: 69 us; the launch traced here: 68.9 us
  Pallas kernels  66.4 us (96%)
  other arithmetic  2.38 us (3%)
    pallas_call x1, Pallas kernels, quadrants_call(): pl.pallas_call(functools.partial(quadrants_kernel, n), out_shape=jax.Shap...  66.4 us
    div x1, other arithmetic, quadrants_call(): return -(integrals + total.astype(F32)) / denominator  2.38 us

profile of v4, /device:TPU:0, one launch (start us, length us, event | category | flops | bytes accessed | tf_op | source)
XLA Modules:
  0.0 68.9 jit_solution(4219960372596331163)
XLA Ops:
  0.0 0.0 copy-start
  0.0 0.0 copy-start.1
  0.0 0.0 copy-start.2
  0.0 66.4 %quadrants.1 = bf16[16,128,128]{2,1,0:T(8,128)(2,1)} custom-call(s32[8,16]{1,0:T(8,128)} %bitcast.3, s32[8,16]{1,0:T(8,128)} %bitcast.4, f32[8,16]{1,0:T(8,128)} %bitcast.5, f32[16]{0:T(128)} %refs_3_.1, bf16[16,128,128]{2,1,0:T(8,128)(2,1)} %refs_4_.1, s32[16,128]{1,0:T(8,128)} %refs_5_.1, f32[16,128,128]{2,1,0:T(8,128)} %refs_6_.1, ...), custom_call_target="tpu_custom_call" | custom-call | tf_op jit(solution)/shard_map/quadrants/pallas_call | solution.py:1152
  66.5 0.0 copy-done
  66.5 0.0 copy-done.1
  66.5 0.0 copy-done.2
  66.5 2.4 %add_divide_fusion = f32[16,128,128]{2,1,0:T(8,128)} fusion(f32[16,128,128]{2,1,0:T(8,128)S(1)} %copy-done, bf16[16,128,128]{2,1,0:T(8,128)(2,1)} %quadrants.1, f32[16]{0:T(128)S(1)} %copy-done.2, f32[16,128]{1,0:T(8,128)S(1)} %copy-done.1), kind=kLoop, calls=%fused_computation | loop fusion | flops 1572864 | bytes 2629696 | tf_op jit(solution)/shard_map/div | solution.py:1188
Async XLA Ops:
  0.0 66.5 %copy-start = (f32[16,128,128]{2,1,0:T(8,128)S(1)}, f32[16,128,128]{2,1,0:T(8,128)}, u32[]{:S(2)}) copy-start(f32[16,128,128]{2,1,0:T(8,128)} %refs_7_.1) | copy-start | bytes 3145732
  0.0 66.5 %copy-start.1 = (f32[16,128]{1,0:T(8,128)S(1)}, f32[16,128]{1,0:T(8,128)}, u32[]{:S(2)}) copy-start(f32[16,128]{1,0:T(8,128)} %refs_8_.1) | copy-start | bytes 24580
  0.0 66.5 %copy-start.2 = (f32[16]{0:T(128)S(1)}, f32[16]{0:T(128)}, u32[]{:S(2)}) copy-start(f32[16]{0:T(128)} %refs_3_.1) | copy-start | bytes 196

commit v5 on v4

--- a/solution.py
+++ b/solution.py
@@ -530,7 +530,7 @@
 def quadrants(
     n, owner_hbm, slot_hbm, fock_hbm, shift_hbm, c_hbm, dom_hbm, start_ref, k_ref, e_hbm, out_ref,
     owner_ref, slot_ref, fock_ref, shift_ref, c_ref, dom_ref, e_ref, src, dom, blocks, bdom, bslot, bfock, wide, turned, x, start, k_own, amps_a, amps_b, amps_c, amps_d,
-    acc, yout, yx, ysum, yin, mine, send, recv, local,
+    acc, yout, yx, ysum, yin, mine, theirs, inverse, send, recv, local,
 ):
     p, g = lax.axis_index("pairs"), lax.axis_index("grp")
     pc, rows, width = c_ref.shape
@@ -835,11 +835,16 @@
         near = yin[it, 1, t].astype(F32)
         return yin[it, 0, t].astype(F32) + jnp.where(mid, near, acc[0, t])
 
+    def invert(t, carry):
+        at_pair = g * quarter + t
+        row = jnp.broadcast_to(e_ref[pl.ds(at_pair, 1), :], (width, width))
+        over = 1.0 / (row.T + row + shift_ref[at_pair])
+        inverse[t] = over
+        k_own[t] = k_own[t] * over
+        return carry
+
     def updated(it, t):
-        at_pair = g * quarter + t
-        total = coupled(it, t)
-        row = jnp.broadcast_to(e_ref[pl.ds(at_pair, 1), :], (width, width))
-        return (-(k_own[t] + total) / (row.T + row + shift_ref[at_pair])).astype(BF16)
+        return (-(k_own[t] + coupled(it, t) * inverse[t])).astype(BF16)
 
     swap_mate, swap_across = (1, 0, 3, 2), (2, 3, 0, 1)
 
@@ -940,7 +945,8 @@
     to_next(2)
     from_mate()
     turn(1)
-    ready(1)
+    ready((1, 0))
+    ready((1, 1))
     wires.wait(("d", 1), dom.at[1])
     wires.wait(("d", 2), dom.at[2])
     wires.start(("d", 3), dom.at[2], dom.at[3], to_mate, "doms")
@@ -961,79 +967,87 @@
     expand(0, 0)
     from_next(0)
     turn(0, 1)
-    next_ready(0)
+    next_ready((0, 0))
+    next_ready((0, 1))
     got_first((0, 1))
     from_across(0)
     turn(2)
     ready((2, 0))
     ready((2, 1))
     from_mate_rest()
+    got_first((1, 0))
     expand(0, 1)
+    from_next(2)
+    got_first((1, 1))
     expand(0, 2, (0,))
-    from_next(2)
-    own_across(1)
-    got_first(1)
     from_across(1)
+    got_further((0, 0))
     from_corner()
     turn(3)
     ready((3, 0))
     ready((3, 1))
     load_start.wait()
     lax.fori_loop(0, pc, cast, 0, unroll=2)
+    for load in (load_k, load_e, load_shift):
+        load.wait()
     wires.wait(("d", 4), dom.at[pl.ds(4, 4)])
     expand(0, 2, (1,))
-    expand(1, 0, (0, 2))
     from_across(2)
     to_wide(2)
     share_start(0)
     share_start(1)
-    got_further(0)
+    got_further((0, 1))
+    expand(1, 0, (0, 2))
     from_next(3)
+    own_across(1)
     expand(0, 2, (2,))
+    got_first((2, 0))
     expand(1, 0, (3,))
-    got_first((2, 0))
     for rel in range(4):
         for t in range(quarter):
             bdom[1, rel * quarter + t] = dom[4 + rel, g * quarter + t]
     next_ready("dom")
     next_ready("slot")
     next_ready("fock")
-    from_next(1)
     from_next_across(0)
     turn(2, 1)
     next_ready((2, 0))
     next_ready((2, 1))
     got_first((2, 1))
+    from_next(1)
     expand(1, 0, (1,))
+    got_first((3, 0))
     from_next_mate()
     turn(1, 1)
     next_ready((1, 0))
     next_ready((1, 1))
-    got_first((3, 0))
     from_next_mate_rest()
-    expand(1, 1)
+    expand(1, 1, (0, 1))
+    from_next_across(1)
     got_first((3, 1))
-    from_across(3)
-    for kind in small:
-        got_first(kind)
-    expand(1, 2, (0,))
-    from_wide(2)
-    got_further((2, 0))
-    expand(0, 2, (3,))
-    expand(1, 2, (2,))
-    from_corner_rest()
-    got_further((2, 1))
-    expand(0, 3)
-    from_next_across(1)
+    expand(1, 1, (2, 3))
     from_next_corner()
     turn(3, 1)
     next_ready((3, 0))
     next_ready((3, 1))
+    for kind in small:
+        got_first(kind)
+    from_wide(2)
+    got_further((2, 0))
+    lax.fori_loop(0, half_quarter, invert, 0)
+    expand(1, 2, (0, 1))
+    from_across(3)
+    got_further((2, 1))
+    expand(1, 2, (2,))
+    expand(0, 2, (3,))
+    from_corner_rest()
+    expand(0, 3, (0, 1))
     got_further((1, 0))
+    expand(0, 3, (2, 3))
+    make_turned(0)
     pass_start(0)
-    expand(1, 2, (1,))
-    make_turned(0)
     got_further((1, 1))
+    lax.fori_loop(half_quarter, quarter, invert, 0)
     from_next_across(3)
     make_x(0, 0)
     expand(1, 2, (3,))
@@ -1071,8 +1085,6 @@
     make_x(0, 1)
     couple(0, 0, 0)
     couple(0, 1, 0)
-    for load in (load_k, load_e, load_shift):
-        load.wait()
     sum_first(0, early)
     sum_second(0)
     sum_first(0, later)
@@ -1094,27 +1106,28 @@
     for t in range(half_quarter, quarter):
         pass_across(t)
     have_partner(1)
-    couple(3, 1, 1)
-    post(1, 1)
-    couple(1, 1, 1)
-    post(1, 0)
+    for b in (3, 1):
+        for ts in (early, later):
+            couple(b, 1, 1, ts)
+            post(1, b // 2, ts)
     couple(2, 1, 1)
     couple(0, 1, 1)
     sum_second(1)
     sum_first(1)
 
     for t in range(quarter):
-        value = coupled(1, t).astype(BF16)
-        mine[t] = value
-        out_ref[g * quarter + t] = value
-        part, dst = mine.at[t], out_ref.at[g * quarter + t]
-        wires.start(("out", 1, t), part, dst, to_across, "amps")
-        wires.start(("out", 2), part, dst, to_mate, "out")
+        mine[t] = coupled(1, t).astype(BF16)
+        part = mine.at[t]
+        wires.start(("out", 1, t), part, theirs.at[t], to_across, "amps")
+        wires.start(("out", 2), part, out_ref.at[g * quarter + t], to_mate, "out")
+    keep_mine = pltpu.make_async_copy(mine, out_ref.at[four(g)], local.at[9])
+    keep_mine.start()
     for t in range(quarter):
-        ref = out_ref.at[across * quarter + t]
+        ref = theirs.at[t]
         wires.wait(("out", 1, t), ref)
-        wires.start(("out", 2), ref, ref, to_mate, "out")
-    wires.wait(("out", 2), both_quarters(out_ref))
+        wires.start(("out", 2), ref, out_ref.at[across * quarter + t], to_mate, "out")
+    keep_theirs = pltpu.make_async_copy(theirs, out_ref.at[four(across)], local.at[10])
+    keep_theirs.start()
     wires.drain("rows", src.at[pl.ds(0, 7)])
     wires.drain("doms", dom.at[pl.ds(0, 7)])
     for role, passes in ((end, 2), (mid, 4)):
@@ -1126,11 +1139,14 @@
     wires.drain("yfar", ysum.at[0])
     wires.drain("ynear", ysum.at[0], mid)
     wires.drain("amps", src.at[pl.ds(0, 3)])
-    wires.drain("out", both_quarters(out_ref))
+    wires.drain("out", both_quarters(amps[1][0]))
+    wires.wait(("out", 2), both_quarters(out_ref))
+    keep_mine.wait()
+    keep_theirs.wait()
     assert len(wires.sends) <= SENDS and len(wires.recvs) <= RECVS, (len(wires.sends), len(wires.recvs))
 
 
-SENDS, RECVS = 11, 110
+SENDS, RECVS = 11, 112
 
 
 def quadrants_fit(n, groups, pc, rows, width):
@@ -1147,13 +1163,13 @@
     pc, rows, width = coefficients.shape
     quarter = pc // 4
     big, ways = (width, width), owner.shape[1]
-    vmem, hbm = pl.BlockSpec(memory_space=pltpu.VMEM), pl.BlockSpec(memory_space=pl.ANY)
+    hbm = pl.BlockSpec(memory_space=pl.ANY)
     dma = pltpu.SemaphoreType.DMA
     total = pl.pallas_call(
         functools.partial(quadrants_kernel, n),
         out_shape=jax.ShapeDtypeStruct((pc, *big), BF16),
         in_specs=[hbm] * 9,
-        out_specs=vmem,
+        out_specs=hbm,
         scratch_shapes=[
             pltpu.SMEM((ways, pc), jnp.int32), pltpu.SMEM((ways, pc), jnp.int32),
             pltpu.SMEM((ways, pc), F32), pltpu.SMEM((pc,), F32),
@@ -1176,8 +1192,9 @@
             pltpu.VMEM((2, 2, quarter, *big), BF16),
             pltpu.VMEM((2, 2, quarter, *big), BF16),
             pltpu.VMEM((2, 2, quarter, *big), BF16),
-            pltpu.VMEM((quarter, *big), BF16),
-            dma((SENDS,)), dma((RECVS,)), dma((9,)),
+            pltpu.VMEM((quarter, *big), BF16), pltpu.VMEM((quarter, *big), BF16),
+            pltpu.VMEM((quarter, *big), F32),
+            dma((SENDS,)), dma((RECVS,)), dma((11,)),
         ],
         compiler_params=pltpu.CompilerParams(
             collective_id=0, has_side_effects=True, vmem_limit_bytes=60 * 2**20

time: 69 us -> 67.7 us (0.981)
  Pallas kernels: 66.4 us -> 65.1 us
    pallas_call x1, Pallas kernels: 66.4 us -> 65.1 us  [quadrants_call(): pl.pallas_call(functools.partial(quadrants_kernel, n), out_shape=jax.Shap...]
where the time goes in v5:
time: 67.7 us; the launch traced here: 67.5 us
  Pallas kernels  65.1 us (96%)
  other arithmetic  2.38 us (4%)
    pallas_call x1, Pallas kernels, quadrants_call(): pl.pallas_call(functools.partial(quadrants_kernel, n), out_shape=jax.Shap...  65.1 us
    div x1, other arithmetic, quadrants_call(): return -(integrals + total.astype(F32)) / denominator  2.38 us

profile of v5, /device:TPU:0, one launch (start us, length us, event | category | flops | bytes accessed | tf_op | source)
XLA Modules:
  0.0 67.5 jit_solution(1814040969990016725)
XLA Ops:
  0.0 0.0 copy-start
  0.0 0.0 copy-start.1
  0.0 0.0 copy-start.2
  0.0 65.1 %quadrants.1 = bf16[16,128,128]{2,1,0:T(8,128)(2,1)} custom-call(s32[8,16]{1,0:T(8,128)} %bitcast.3, s32[8,16]{1,0:T(8,128)} %bitcast.4, f32[8,16]{1,0:T(8,128)} %bitcast.5, f32[16]{0:T(128)} %refs_3_.1, bf16[16,128,128]{2,1,0:T(8,128)(2,1)} %refs_4_.1, s32[16,128]{1,0:T(8,128)} %refs_5_.1, f32[16,128,128]{2,1,0:T(8,128)} %refs_6_.1, ...), custom_call_target="tpu_custom_call" | custom-call | tf_op jit(solution)/shard_map/quadrants/pallas_call | solution.py:1168
  65.1 0.0 copy-done
  65.1 0.0 copy-done.1
  65.1 0.0 copy-done.2
  65.1 2.4 %add_divide_fusion = f32[16,128,128]{2,1,0:T(8,128)} fusion(f32[16,128,128]{2,1,0:T(8,128)S(1)} %copy-done, bf16[16,128,128]{2,1,0:T(8,128)(2,1)} %quadrants.1, f32[16]{0:T(128)S(1)} %copy-done.2, f32[16,128]{1,0:T(8,128)S(1)} %copy-done.1), kind=kLoop, calls=%fused_computation | loop fusion | flops 1572864 | bytes 2629696 | tf_op jit(solution)/shard_map/div | solution.py:1205
Async XLA Ops:
  0.0 65.1 %copy-start = (f32[16,128,128]{2,1,0:T(8,128)S(1)}, f32[16,128,128]{2,1,0:T(8,128)}, u32[]{:S(2)}) copy-start(f32[16,128,128]{2,1,0:T(8,128)} %refs_7_.1) | copy-start | bytes 3145732
  0.0 65.1 %copy-start.1 = (f32[16,128]{1,0:T(8,128)S(1)}, f32[16,128]{1,0:T(8,128)}, u32[]{:S(2)}) copy-start(f32[16,128]{1,0:T(8,128)} %refs_8_.1) | copy-start | bytes 24580
  0.0 65.1 %copy-start.2 = (f32[16]{0:T(128)S(1)}, f32[16]{0:T(128)}, u32[]{:S(2)}) copy-start(f32[16]{0:T(128)} %refs_3_.1) | copy-start | bytes 196

commit v6 on v5

--- a/solution.py
+++ b/solution.py
@@ -813,8 +813,8 @@
     def have_partner(it):
         wires.wait(("a", it, 2), both_quarters(amps[it][1]))
 
-    def sum_second(it):
-        for t in range(quarter):
+    def sum_second(it, ts=every):
+        for t in ts:
             wires.wait(("y", it, 1, t), yx.at[it, 1, t])
             ysum[it, 1, t] = (acc[2, t] + yx[it, 1, t].astype(F32)).astype(BF16)
             job = (("yfar", it, t), ysum.at[it, 1, t], yin.at[it, 0, t])
@@ -1106,14 +1106,16 @@
     for t in range(half_quarter, quarter):
         pass_across(t)
     have_partner(1)
-    for b in (3, 1):
-        for ts in (early, later):
+    for ts in (early, later):
+        for b in (3, 1):
             couple(b, 1, 1, ts)
             post(1, b // 2, ts)
     couple(2, 1, 1)
     couple(0, 1, 1)
-    sum_second(1)
-    sum_first(1)
+    sum_second(1, early)
+    sum_first(1, early)
+    sum_second(1, later)
+    sum_first(1, later)
 
     for t in range(quarter):
         mine[t] = coupled(1, t).astype(BF16)

time: 67.7 us -> 67.4 us (level)
  no operation moved by 1% of the time
where the time goes in v6:
time: 67.4 us; the launch traced here: 67.2 us
  Pallas kernels  64.8 us (96%)
  other arithmetic  2.38 us (4%)
    pallas_call x1, Pallas kernels, quadrants_call(): pl.pallas_call(functools.partial(quadrants_kernel, n), out_shape=jax.Shap...  64.8 us
    div x1, other arithmetic, quadrants_call(): return -(integrals + total.astype(F32)) / denominator  2.38 us

profile of v6, /device:TPU:0, one launch (start us, length us, event | category | flops | bytes accessed | tf_op | source)
XLA Modules:
  0.0 67.2 jit_solution(17817440923203792349)
XLA Ops:
  0.0 0.0 copy-start
  0.0 0.0 copy-start.1
  0.0 0.0 copy-start.2
  0.0 64.8 %quadrants.1 = bf16[16,128,128]{2,1,0:T(8,128)(2,1)} custom-call(s32[8,16]{1,0:T(8,128)} %bitcast.3, s32[8,16]{1,0:T(8,128)} %bitcast.4, f32[8,16]{1,0:T(8,128)} %bitcast.5, f32[16]{0:T(128)} %refs_3_.1, bf16[16,128,128]{2,1,0:T(8,128)(2,1)} %refs_4_.1, s32[16,128]{1,0:T(8,128)} %refs_5_.1, f32[16,128,128]{2,1,0:T(8,128)} %refs_6_.1, ...), custom_call_target="tpu_custom_call" | custom-call | tf_op jit(solution)/shard_map/quadrants/pallas_call | solution.py:1170
  64.8 0.0 copy-done
  64.8 0.0 copy-done.1
  64.8 0.0 copy-done.2
  64.9 2.4 %add_divide_fusion = f32[16,128,128]{2,1,0:T(8,128)} fusion(f32[16,128,128]{2,1,0:T(8,128)S(1)} %copy-done, bf16[16,128,128]{2,1,0:T(8,128)(2,1)} %quadrants.1, f32[16]{0:T(128)S(1)} %copy-done.2, f32[16,128]{1,0:T(8,128)S(1)} %copy-done.1), kind=kLoop, calls=%fused_computation | loop fusion | flops 1572864 | bytes 2629696 | tf_op jit(solution)/shard_map/div | solution.py:1207
Async XLA Ops:
  0.0 64.8 %copy-start = (f32[16,128,128]{2,1,0:T(8,128)S(1)}, f32[16,128,128]{2,1,0:T(8,128)}, u32[]{:S(2)}) copy-start(f32[16,128,128]{2,1,0:T(8,128)} %refs_7_.1) | copy-start | bytes 3145732
  0.0 64.8 %copy-start.1 = (f32[16,128]{1,0:T(8,128)S(1)}, f32[16,128]{1,0:T(8,128)}, u32[]{:S(2)}) copy-start(f32[16,128]{1,0:T(8,128)} %refs_8_.1) | copy-start | bytes 24580
  0.0 64.8 %copy-start.2 = (f32[16]{0:T(128)S(1)}, f32[16]{0:T(128)}, u32[]{:S(2)}) copy-start(f32[16]{0:T(128)} %refs_3_.1) | copy-start | bytes 196

commit v7 on v6

--- a/solution.py
+++ b/solution.py
@@ -699,7 +699,7 @@
 
         if len(parts) == 4:
             note("expand", b, rel)
-            lax.fori_loop(0, pc, one, 0, unroll=4)
+            lax.fori_loop(0, pc, one, 0, unroll=8)
             return
         for i in parts:
             note("expand4", b, rel)

time: 67.4 us -> 67.7 us (level)
  no operation moved by 1% of the time
where the time goes in v7:
time: 67.7 us; the launch traced here: 67.5 us
  Pallas kernels  65.1 us (96%)
  other arithmetic  2.38 us (4%)
    pallas_call x1, Pallas kernels, quadrants_call(): pl.pallas_call(functools.partial(quadrants_kernel, n), out_shape=jax.Shap...  65.1 us
    div x1, other arithmetic, quadrants_call(): return -(integrals + total.astype(F32)) / denominator  2.38 us

profile of v7, /device:TPU:0, one launch (start us, length us, event | category | flops | bytes accessed | tf_op | source)
XLA Modules:
  0.0 67.5 jit_solution(13479309426478451474)
XLA Ops:
  0.0 0.0 copy-start
  0.0 0.0 copy-start.1
  0.0 0.0 copy-start.2
  0.0 65.1 %quadrants.1 = bf16[16,128,128]{2,1,0:T(8,128)(2,1)} custom-call(s32[8,16]{1,0:T(8,128)} %bitcast.3, s32[8,16]{1,0:T(8,128)} %bitcast.4, f32[8,16]{1,0:T(8,128)} %bitcast.5, f32[16]{0:T(128)} %refs_3_.1, bf16[16,128,128]{2,1,0:T(8,128)(2,1)} %refs_4_.1, s32[16,128]{1,0:T(8,128)} %refs_5_.1, f32[16,128,128]{2,1,0:T(8,128)} %refs_6_.1, ...), custom_call_target="tpu_custom_call" | custom-call | tf_op jit(solution)/shard_map/quadrants/pallas_call | solution.py:1170
  65.1 0.0 copy-done
  65.1 0.0 copy-done.1
  65.1 0.0 copy-done.2
  65.1 2.4 %add_divide_fusion = f32[16,128,128]{2,1,0:T(8,128)} fusion(f32[16,128,128]{2,1,0:T(8,128)S(1)} %copy-done, bf16[16,128,128]{2,1,0:T(8,128)(2,1)} %quadrants.1, f32[16]{0:T(128)S(1)} %copy-done.2, f32[16,128]{1,0:T(8,128)S(1)} %copy-done.1), kind=kLoop, calls=%fused_computation | loop fusion | flops 1572864 | bytes 2629696 | tf_op jit(solution)/shard_map/div | solution.py:1207
Async XLA Ops:
  0.0 65.1 %copy-start = (f32[16,128,128]{2,1,0:T(8,128)S(1)}, f32[16,128,128]{2,1,0:T(8,128)}, u32[]{:S(2)}) copy-start(f32[16,128,128]{2,1,0:T(8,128)} %refs_7_.1) | copy-start | bytes 3145732
  0.0 65.1 %copy-start.1 = (f32[16,128]{1,0:T(8,128)S(1)}, f32[16,128]{1,0:T(8,128)}, u32[]{:S(2)}) copy-start(f32[16,128]{1,0:T(8,128)} %refs_8_.1) | copy-start | bytes 24580
  0.0 65.1 %copy-start.2 = (f32[16]{0:T(128)S(1)}, f32[16]{0:T(128)}, u32[]{:S(2)}) copy-start(f32[16]{0:T(128)} %refs_3_.1) | copy-start | bytes 196
